TPU v7x, 32 devices: a whole 2x2x4 slice. The times are simulated.
32 devices in a mesh: micro: 4 (over z), grid: 8 (over y, x, core).
Axes of the slice: x: 2, y: 2, z: 4, core: 2. Of those that a mesh axis runs over, the one named last changes fastest.
Arguments:
- orbitals: float32 [2, 32, 64, 16, 256], P(None, 'micro', None, 'grid'), may hold values from -14 to 14
- local_potential: float32 [32, 16, 256], P('micro', 'grid'), may hold values from -1 to 1
- projectors: float32 [2, 32, 16, 256], P(None, None, 'grid'), may hold values from -0.09375 to 0.09375
- strengths: float32 [2, 32], replicated, may hold values from 1 to 12
- material: int32 [32], replicated, may hold values from 0 to 1
- proj_kind: int32 [32], replicated, may hold values from 0 to 1
- point_cell: int32 [32], replicated, may hold values from 0 to 1999
- vector_now: float32 [2000], replicated, may hold values from -3 to 3
- vector_old: float32 [2000], replicated, may hold values from -3 to 3
Outputs:
- orbitals_out: float32 [2, 32, 64, 16, 256], P(None, 'micro', None, 'grid')
- vector_field: float32 [2000], replicated
All inputs are finite; a program needn't handle non-finite values.
Results may differ from a plain program's by a relative error of at most 0.0003.
Values sent between devices are 32-bit elements; how exact they have to be, the bound alone decides.
A program may use at most 128 MiB of HBM per device.

v0:
```python
import functools

import jax
import jax.numpy as jnp
from jax import lax
from jax.experimental import pallas as pl
from jax.experimental.pallas import tpu as pltpu
from jax.sharding import PartitionSpec as P

NZ = 16
STEPS = 2
ORDER = 4
BLOCK = 8
SMALL = 4
GROUPS = 1

SPACING = 0.64
TIME_STEP = 0.05
COURANT = 0.9
COUPLING = 1.0
HIGHEST = lax.Precision.HIGHEST
F32 = jnp.float32
BF16 = jnp.bfloat16


def split(value):
    high = value.astype(BF16)
    low = (value - high.astype(F32)).astype(BF16)
    return jnp.concatenate([high, low], axis=-1)


def stencil_matrix(cells):
    row = lax.broadcasted_iota(jnp.int32, (cells, cells), 0)
    col = lax.broadcasted_iota(jnp.int32, (cells, cells), 1)
    z = col % NZ
    forward = row == (col - z + (z + 1) % NZ)
    backward = row == (col - z + (z + NZ - 1) % NZ)
    y_next = row == (col + NZ) % cells
    y_last = row == (col + cells - NZ) % cells
    one = lambda m: m.astype(F32)
    beside = one(forward) + one(backward) + one(y_next) + one(y_last)
    both = jnp.concatenate([beside, one(forward) - one(backward)], axis=1)
    return jnp.concatenate([both, both], axis=0).astype(BF16)


def nt_dot(left, right):
    return lax.dot_general(left, right, (((1,), (1,)), ((), ())), preferred_element_type=F32)


def macro_update(present, previous, deposit, macro):
    high, lanes = present.shape
    lane = lax.broadcasted_iota(jnp.int32, present.shape, 1)
    flat = lax.broadcasted_iota(jnp.int32, present.shape, 0) * lanes + lane
    ahead = pltpu.roll(present, lanes - 1, 1)
    ahead = jnp.where(lane == lanes - 1, pltpu.roll(ahead, high - 1, 0), ahead)
    behind = pltpu.roll(present, 1, 1)
    behind = jnp.where(lane == 0, pltpu.roll(behind, 1, 0), behind)
    curvature = ahead + behind - 2.0 * present
    following = 2.0 * present - previous + COURANT**2 * curvature - COUPLING * deposit
    return jnp.where(flat < macro, following, 0.0)


def kernel(
    norm, macro, share, grid, devices,
    material_ref, kind_ref, cell_ref, packed_ref, packed_side_ref, weight_ref, stencil_ref, mix_ref, now_ref, old_ref,
    out_ref, vector_ref,
    total_ref, side_ref, term_a, term_b, parts_ref, back_ref, fore_ref, overlap_ref, previous_ref,
    mine_ref, currents_ref, send_sem, recv_sem,
    in_send, in_recv, side_send, side_recv, out_send, out_recv, own_sem,
):
    groups, planes, rows, cells = total_ref.shape
    mine = planes // grid
    half = rows // 2
    nproj = mix_ref.shape[0] // 4
    k2 = 1.0 / (2.0 * SPACING**2)
    here = lax.axis_index("grid")
    layer = lax.axis_index("micro")
    me = layer * grid + here
    own = groups * half
    first_orbital = lax.rem(here, share) * own
    limit = jnp.where(material_ref[me] == 1, share * own, share * own // 2) - first_orbital
    my_cell, my_kind = cell_ref[me], kind_ref[me]
    weight = jnp.where(my_kind == 0, weight_ref[0:1, :], 0.0)
    for kind in range(1, weight_ref.shape[0]):
        weight = weight + jnp.where(my_kind == kind, weight_ref[kind:kind + 1, :], 0.0)
    barrier = pltpu.get_barrier_semaphore()

    def peer(distance):
        other = lax.rem(me + distance, devices)
        return other, (other // grid, lax.rem(other, grid))

    def beside_me(distance):
        return lax.rem(here + distance, grid)

    def remote(source, target, sent, received, device):
        return pltpu.make_async_remote_copy(
            src_ref=source, dst_ref=target, send_sem=sent, recv_sem=received,
            device_id=device, device_id_type=pl.DeviceIdType.MESH,
        )

    def planes_of(owner):
        return pl.ds(owner * mine, mine)

    def side_copy(distance, owner):
        other = beside_me(distance)
        return remote(
            packed_side_ref.at[other], side_ref.at[planes_of(owner)],
            side_send.at[distance], side_recv.at[owner], (layer, other),
        )

    def in_copy(group, distance, owner):
        other = beside_me(distance)
        return remote(
            packed_ref.at[group, other], total_ref.at[group, planes_of(owner)],
            in_send.at[group, distance], in_recv.at[group, owner], (layer, other),
        )

    def out_copy(group, distance, owner):
        other = beside_me(distance)
        return remote(
            total_ref.at[group, planes_of(other)], out_ref.at[group, owner],
            out_send.at[group, distance], out_recv.at[group, owner], (layer, other),
        )

    def own_side():
        return pltpu.make_async_copy(packed_side_ref.at[here], side_ref.at[planes_of(here)], own_sem.at[0])

    def own_in(group):
        return pltpu.make_async_copy(
            packed_ref.at[group, here], total_ref.at[group, planes_of(here)], own_sem.at[1 + group]
        )

    def own_out(group):
        return pltpu.make_async_copy(
            total_ref.at[group, planes_of(here)], out_ref.at[group, here], own_sem.at[1 + groups + group]
        )

    @pl.loop(1, devices)
    def _(distance):
        pl.semaphore_signal(barrier, inc=1, device_id=peer(distance)[1], device_id_type=pl.DeviceIdType.MESH)

    own_side().start()
    for group in range(groups):
        own_in(group).start()
    vector_ref[...] = now_ref[...]
    previous_ref[...] = old_ref[...]
    pl.semaphore_wait(barrier, devices - 1)

    @pl.loop(1, grid)
    def _(distance):
        side_copy(distance, here).start()

    for group in range(groups):
        @pl.loop(1, grid)
        def _(distance):
            in_copy(group, distance, here).start()

    own_side().wait()

    @pl.loop(1, grid)
    def _(distance):
        side_copy(distance, here).wait_send()
        side_copy(distance, beside_me(distance)).wait_recv()

    def prepare(x, carry):
        beta = side_ref[x, :nproj, :]
        high = beta.astype(BF16).astype(F32)
        low = beta - high
        zero = jnp.zeros_like(high)
        back_ref[x] = jnp.concatenate([high, high, low, zero], axis=0).astype(BF16)
        fore = jnp.concatenate([high, low, zero, zero], axis=0).astype(BF16)
        fore_ref[x] = jnp.concatenate([fore, fore], axis=1)
        return carry

    lax.fori_loop(0, planes, prepare, 0, unroll=SMALL)
    none = jnp.zeros((rows, 4 * nproj), F32)
    lane = lax.broadcasted_iota(jnp.int32, (rows, 4 * nproj), 1)
    middle = (lane >= nproj) & (lane < 2 * nproj)
    row_id = lax.broadcasted_iota(jnp.int32, (half, 1), 0)
    flat = (
        lax.broadcasted_iota(jnp.int32, now_ref.shape, 0) * now_ref.shape[1]
        + lax.broadcasted_iota(jnp.int32, now_ref.shape, 1)
    )

    def advance_group(step, group, a):
        occupied = jnp.where(row_id + group * half < limit, 1.0, 0.0).astype(F32)

        @pl.when(step == 0)
        def _():
            own_in(group).wait()

            @pl.loop(1, grid)
            def _(distance):
                in_copy(group, distance, here).wait_send()
                in_copy(group, distance, beside_me(distance)).wait_recv()

            def setup(x, overlap):
                value = total_ref[group, x]
                term_b[group, x] = value
                pieces = split(value)
                parts_ref[group, x] = pieces
                return overlap + nt_dot(pieces, fore_ref[x])

            overlap_ref[group] = lax.fori_loop(0, planes, setup, none, unroll=SMALL)

        overlap = overlap_ref[group]
        source = term_b
        for degree in range(1, ORDER + 1):
            target = term_a if degree % 2 == 1 else term_b
            scale = TIME_STEP / degree
            c = jnp.dot(overlap, mix_ref[...], precision=HIGHEST, preferred_element_type=F32) * weight
            high = c.astype(BF16).astype(F32)
            coefficients = jnp.where(middle, c - high, high).astype(BF16)
            base = 3.0 / SPACING**2 + 0.5 * a * a

            def body(block, overlap, source=source, target=target, scale=scale, coefficients=coefficients, degree=degree):
                x0 = block * BLOCK
                pieces = parts_ref[group, pl.ds(x0, BLOCK)].reshape(BLOCK * rows, 2 * cells)
                stencils = jnp.dot(pieces, stencil_ref[...], preferred_element_type=F32)
                for offset in range(BLOCK):
                    x = x0 + offset
                    up = lax.rem(x + 1, planes)
                    down = lax.rem(x + planes - 1, planes)
                    both = stencils[offset * rows:(offset + 1) * rows]
                    nonlocal_part = jnp.dot(coefficients, back_ref[x], preferred_element_type=F32)
                    beside = both[:, :cells] + nonlocal_part + (source[group, up] + source[group, down])
                    drift = both[:, cells:] * (a * (scale / (2.0 * SPACING)))
                    diag = (side_ref[x, nproj:nproj + 1, :] + base) * scale
                    kinetic = diag * source[group, x] - beside * (k2 * scale)
                    new = jnp.concatenate([kinetic[half:] - drift[:half], -kinetic[:half] - drift[half:]], axis=0)
                    summed = total_ref[group, x] + new
                    total_ref[group, x] = summed
                    term = new if degree < ORDER else summed
                    target[group, x] = term
                    pieces = split(term)
                    parts_ref[group, x] = pieces
                    overlap = overlap + nt_dot(pieces, fore_ref[x])
                return overlap

            overlap = lax.fori_loop(0, planes // BLOCK, body, none)
            source = target
        overlap_ref[group] = overlap

        @pl.when(step == STEPS - 1)
        def _():
            def mask(x, carry):
                total_ref[group, x, :half, :] = total_ref[group, x, :half, :] * occupied
                total_ref[group, x, half:, :] = total_ref[group, x, half:, :] * occupied
                return carry

            lax.fori_loop(0, planes, mask, 0, unroll=SMALL)

            @pl.loop(1, grid)
            def _(distance):
                out_copy(group, distance, here).start()

            own_out(group).start()

        def current(x, acc):
            gradient = jnp.dot(parts_ref[group, x], stencil_ref[:, cells:], preferred_element_type=F32) * (0.5 / SPACING)
            value = term_b[group, x]
            real, imag = value[:half], value[half:]
            return acc + (
                real * gradient[half:] - imag * gradient[:half] + a * (real * real + imag * imag)
            )

        acc = lax.fori_loop(0, planes, current, jnp.zeros((half, cells), F32), unroll=SMALL)
        return jnp.sum(acc * occupied, axis=0, keepdims=True)

    def copy(step, distance, owner):
        return remote(
            mine_ref.at[step], currents_ref.at[step, owner],
            send_sem.at[step, distance], recv_sem.at[step, owner], peer(distance)[1],
        )

    def advance(step, carry):
        a = jnp.sum(jnp.where(flat == my_cell, vector_ref[...], 0.0))
        acc = advance_group(step, 0, a)
        for group in range(1, groups):
            acc = acc + advance_group(step, group, a)
        mine_ref[step] = jnp.full((1, 128), jnp.sum(acc) * norm, F32)

        @pl.loop(1, devices)
        def _(distance):
            copy(step, distance, me).start()

        currents_ref[step, me] = mine_ref[step]

        @pl.loop(1, devices)
        def _(distance):
            copy(step, distance, me).wait_send()
            copy(step, distance, peer(distance)[0]).wait_recv()

        def add(source, deposit):
            return deposit + jnp.where(flat == cell_ref[source], currents_ref[step, source], 0.0)

        deposit = lax.fori_loop(0, devices, add, jnp.zeros(flat.shape, F32), unroll=SMALL)
        present = vector_ref[...]
        vector_ref[...] = macro_update(present, previous_ref[...], deposit, macro)
        previous_ref[...] = present
        return carry

    lax.fori_loop(0, STEPS, advance, 0)
    for group in range(groups):
        own_out(group).wait()

        @pl.loop(1, grid)
        def _(distance):
            out_copy(group, distance, here).wait_send()
            out_copy(group, distance, beside_me(distance)).wait_recv()


def propagate(materials, kinds, owners, packed, side, weights, stencil, mix, now, old, norm, macro, share, grid, devices):
    groups, _, mine, rows, cells = packed.shape
    planes = grid * mine
    assert planes % BLOCK == 0
    vmem = pl.BlockSpec(memory_space=pltpu.VMEM)
    smem = pl.BlockSpec(memory_space=pltpu.SMEM)
    anywhere = pl.BlockSpec(memory_space=pl.ANY)
    return pl.pallas_call(
        functools.partial(kernel, norm, macro, share, grid, devices),
        out_shape=(
            jax.ShapeDtypeStruct(packed.shape, F32),
            jax.ShapeDtypeStruct(now.shape, F32),
        ),
        in_specs=[smem] * 3 + [anywhere] * 2 + [vmem] * 5,
        out_specs=(anywhere, vmem),
        scratch_shapes=[
            pltpu.VMEM((groups, planes, rows, cells), F32),
            pltpu.VMEM((planes,) + side.shape[2:], F32),
            pltpu.VMEM((groups, planes, rows, cells), F32),
            pltpu.VMEM((groups, planes, rows, cells), F32),
            pltpu.VMEM((groups, planes, rows, 2 * cells), BF16),
            pltpu.VMEM((planes, mix.shape[0], cells), BF16),
            pltpu.VMEM((planes, mix.shape[0], 2 * cells), BF16),
            pltpu.VMEM((groups, rows, mix.shape[0]), F32),
            pltpu.VMEM(now.shape, F32),
            pltpu.VMEM((STEPS, 1, 128), F32),
            pltpu.VMEM((STEPS, devices, 1, 128), F32),
            pltpu.SemaphoreType.DMA((STEPS, devices)),
            pltpu.SemaphoreType.DMA((STEPS, devices)),
            pltpu.SemaphoreType.DMA((groups, grid)),
            pltpu.SemaphoreType.DMA((groups, grid)),
            pltpu.SemaphoreType.DMA((grid,)),
            pltpu.SemaphoreType.DMA((grid,)),
            pltpu.SemaphoreType.DMA((groups, grid)),
            pltpu.SemaphoreType.DMA((groups, grid)),
            pltpu.SemaphoreType.DMA((1 + 2 * groups,)),
        ],
        compiler_params=pltpu.CompilerParams(
            vmem_limit_bytes=48 * 1024 * 1024, collective_id=0, has_side_effects=True
        ),
        name="propagate",
    )(materials, kinds, owners, packed, side, weights, stencil, mix, now, old)


def local(
    orbitals, local_potential, projectors, strengths, material, proj_kind, point_cell,
    vector_now, vector_old, devices, grid,
):
    _, points, orb, mine, cells = orbitals.shape
    assert grid % points == 0 and orb % (grid // points) == 0
    share = grid // points
    own = orb // share
    nproj = projectors.shape[1]
    first_point = lax.axis_index("micro") * points
    kinds = lax.dynamic_slice_in_dim(proj_kind, first_point, points)
    repeat = lambda array: jnp.repeat(array, share, axis=0)
    packed = (
        orbitals.reshape(2, points, share, GROUPS, own // GROUPS, mine, cells)
        .transpose(3, 1, 2, 5, 0, 4, 6)
        .reshape(GROUPS, grid, mine, 2 * own // GROUPS, cells)
    )
    side = repeat(
        jnp.concatenate(
            [
                jnp.take(projectors, kinds, axis=0, mode="clip").transpose(0, 2, 1, 3),
                jnp.broadcast_to(local_potential[:, :, None, :], (points, mine, 8, cells)),
            ],
            axis=2,
        )
    )
    scaled = strengths * (-2.0 * SPACING**2)
    weights = jnp.concatenate([scaled] * 3 + [jnp.zeros_like(scaled)], axis=1)
    i = lax.broadcasted_iota(jnp.int32, (4 * nproj, 4 * nproj), 0)
    j = lax.broadcasted_iota(jnp.int32, (4 * nproj, 4 * nproj), 1)
    mix = ((i < 2 * nproj) & (i % nproj == j % nproj)).astype(F32)
    stencil = stencil_matrix(cells)
    macro = vector_now.shape[0]
    wide = (macro // 1024 + 1) * 1024
    lay = lambda vector: jnp.pad(vector, (0, wide - macro)).reshape(-1, 128)
    field, vector = propagate(
        repeat(material), repeat(proj_kind), repeat(point_cell), packed, side, weights, stencil, mix, lay(vector_now), lay(vector_old),
        2.0 / (orb * grid * mine * cells), macro, share, grid, devices,
    )
    field = field.reshape(GROUPS, points, share, mine, 2, own // GROUPS, cells).transpose(4, 1, 2, 0, 5, 3, 6)
    field = field.reshape(2, points, orb, mine, cells)
    return field, vector.reshape(-1)[:macro]


def solution(mesh):
    in_specs = (
        P(None, "micro", None, "grid", None),
        P("micro", "grid", None),
        P(None, None, "grid", None),
        P(),
        P(),
        P(),
        P(),
        P(),
        P(),
    )
    out_specs = (P(None, "micro", None, "grid", None), P())
    body = functools.partial(local, devices=mesh.size, grid=mesh.shape["grid"])
    return jax.shard_map(body, mesh=mesh, in_specs=in_specs, out_specs=out_specs, check_vma=False)
```

profile of v0, /device:TPU:0, one launch (start us, length us, event | category | flops | bytes accessed | tf_op | source)
XLA Modules:
  0.0 110.7 jit_solution(16383856186968165052)
XLA Ops:
  0.6 0.0 copy-start
  0.6 0.8 dynamic_slice.3
  1.4 0.1 pad.16.clone
  1.5 0.7 broadcast_multiply_fusion
  2.2 0.1 maximum_maximum_fusion.weight_ref
  2.3 0.7 pad_bitcast_fusion
  3.0 0.1 fusion.13.mix_ref
  3.2 0.7 broadcast_in_dim.14
  3.9 0.2 fusion.7
  4.1 0.0 copy-start.4
  4.2 0.0 copy-done
  4.2 1.1 %gather_fusion = f32[8,32,2,256]{3,2,1,0:T(2,128)S(1)} fusion(f32[2,32,2,256]{3,2,1,0:T(2,128)S(1)} %copy-done, s32[1024]{0:T(1024)S(1)} %pad_clamp_fusion), kind=kCustom, calls=%fused_computation | custom fusion | bytes 1048608 | tf_op jit(solution)/shard_map/jit(_take)/gather | solution.py:377
  5.3 0.1 copy.19
  5.3 0.1 pad_maximum_fusion.packed_side_ref
  5.4 0.3 copy-done.4
  5.7 0.0 copy-start.1
  5.7 0.0 copy-start.2
  5.7 0.0 copy-start.3
  5.7 0.3 copy.13
  6.0 0.4 copy-done.1
  6.4 0.0 copy-done.2
  6.4 0.0 copy-done.3
  6.4 100.8 %propagate.1 = (f32[1,8,2,128,256]{4,3,2,1,0:T(8,128)S(1)}, f32[16,128]{1,0:T(8,128)S(1)}) custom-call(s32[32]{0:T(128)S(1)} %copy-done.1, s32[32]{0:T(128)S(1)} %copy-done.2, s32[32]{0:T(128)S(1)} %copy-done.3, f32[1,8,2,128,256]{4,3,2,1,0:T(8,128)S(1)} %bitcast.19, f32[8,2,40,256]{3,2,1,0:T(8,128)S(1)} %pad_maximum_fusion.packed_side_ref, ...), custom_call_target="tpu_custom_call" | custom-call | tf_op jit(solution)/shard_map/propagate/pallas_call | solution.py:320
  107.1 3.0 %copy.18 = f32[1,8,1,2,2,64,256]{6,3,5,1,4,0,2:T(2,128)} copy(f32[1,8,1,2,2,64,256]{6,5,4,3,1,2,0:T(8,128)S(1)} %bitcast.20) | data formatting | bytes 4194304 | tf_op jit(solution)/shard_map/reshape | solution.py:396
  110.1 0.6 copy.21
  (11 shorter events, 0.1 us)
Async XLA Ops:
  0.6 3.5 %copy-start = (f32[2,32,2,256]{3,2,1,0:T(2,128)S(1)}, f32[2,32,2,256]{3,2,1,0:T(2,128)}, u32[]{:S(2)}) copy-start(f32[2,32,2,256]{3,2,1,0:T(2,128)} %param.11) | copy-start | bytes 393220
  4.1 1.6 %copy-start.4 = (f32[2,8,64,2,256]{4,3,2,1,0:T(2,128)S(1)}, f32[2,8,64,2,256]{4,3,2,1,0:T(2,128)}, u32[]{:S(2)}) copy-start(f32[2,8,64,2,256]{4,3,2,1,0:T(2,128)} %param.9) | copy-start | bytes 6291460
  5.7 0.7 copy-start.1
  5.7 0.7 copy-start.2
  5.7 0.7 copy-start.3
where the time goes:
time: 111 us
  Pallas kernels  101 us (91%)
  local copies, waits for them, and re-layouts  7.99 us (7%)
  other arithmetic  1.2 us (1%)
    pallas_call x1, Pallas kernels, propagate(): pl.pallas_call(functools.partial(kernel, norm, macro, share, grid, device...  101 us
    reshape x1, local copies, waits for them, and re-layouts, local(): field.reshape(GROUPS, points, share, mine, 2, own // GROUPS, cells)  2.96 us

commit v1 on v0

v1 whole, which is shorter than its diff:
```python
import functools

import jax
import jax.numpy as jnp
from jax import lax
from jax.experimental import pallas as pl
from jax.experimental.pallas import tpu as pltpu
from jax.sharding import PartitionSpec as P

NZ = 16
STEPS = 2
ORDER = 4
LANES = 128
GROUPS = 2

SPACING = 0.64
TIME_STEP = 0.05
COURANT = 0.9
COUPLING = 1.0
F32 = jnp.float32
BF16 = jnp.bfloat16


def halves(value):
    high = value.astype(BF16)
    return high, (value - high.astype(F32)).astype(BF16)


def macro_update(present, previous, deposit, macro):
    high, lanes = present.shape
    lane = lax.broadcasted_iota(jnp.int32, present.shape, 1)
    flat = lax.broadcasted_iota(jnp.int32, present.shape, 0) * lanes + lane
    ahead = pltpu.roll(present, lanes - 1, 1)
    ahead = jnp.where(lane == lanes - 1, pltpu.roll(ahead, high - 1, 0), ahead)
    behind = pltpu.roll(present, 1, 1)
    behind = jnp.where(lane == 0, pltpu.roll(behind, 1, 0), behind)
    curvature = ahead + behind - 2.0 * present
    following = 2.0 * present - previous + COURANT**2 * curvature - COUPLING * deposit
    return jnp.where(flat < macro, following, 0.0)


def kernel(
    norm, macro, share, grid, layers, mine, own,
    material_ref, kind_ref, cell_ref, strength_ref, projector_ref, potential_ref, now_ref, old_ref, field_ref,
    out_ref, vector_ref,
    terms_ref, land_ref, parts_ref, packed_ref, side_ref, fore_ref, back_ref, diag_ref, weight_ref, previous_ref,
    row_ref, rows_ref, all_ref,
    in_send, in_recv, side_send, side_recv, out_send, out_recv, row_send, row_recv, all_send, all_recv, own_sem,
):
    _, groups, slots, cells, lanes = terms_ref.shape
    slots = slots - 2
    kinds, nproj = strength_ref.shape
    points = potential_ref.shape[0]
    per = potential_ref.shape[1]
    wide = cells // lanes
    orbs = own // groups
    blocks = lanes // (2 * orbs)
    here = lax.axis_index("grid")
    layer = lax.axis_index("micro")
    my_point = lax.div(here, share)
    first_orbital = lax.rem(here, share) * own
    me = layer * points + my_point
    limit = jnp.where(material_ref[me] == 1, share * own, share * own // 2) - first_orbital
    my_cell, my_kind = cell_ref[me], kind_ref[me]
    barrier = pltpu.get_barrier_semaphore()
    piece = orbs * per

    def beside_me(distance):
        return lax.rem(here + distance, grid)

    def above_me(distance):
        return lax.rem(layer + distance, layers)

    def remote(source, target, sent, received, device):
        return pltpu.make_async_remote_copy(
            src_ref=source, dst_ref=target, send_sem=sent, recv_sem=received,
            device_id=device, device_id_type=pl.DeviceIdType.MESH,
        )

    def field_part(ref, group, device):
        first = (lax.rem(device, share) * own + group * orbs) * per
        return ref.at[:, lax.div(device, share), pl.ds(pl.multiple_of(first, 8), piece), :]

    def side_copy(distance, owner):
        other = beside_me(distance)
        return remote(
            packed_ref.at[other], side_ref.at[owner], side_send.at[distance], side_recv.at[owner], (layer, other)
        )

    def in_copy(group, distance, owner):
        other = beside_me(distance)
        return remote(
            field_part(field_ref, group, other), land_ref.at[group, owner],
            in_send.at[group, distance], in_recv.at[group, owner], (layer, other),
        )

    def out_copy(group, distance, owner):
        other = beside_me(distance)
        return remote(
            land_ref.at[group, other], field_part(out_ref, group, owner),
            out_send.at[group, distance], out_recv.at[group, owner], (layer, other),
        )

    def own_side():
        return pltpu.make_async_copy(packed_ref.at[here], side_ref.at[here], own_sem.at[0])

    def own_in(group):
        return pltpu.make_async_copy(field_part(field_ref, group, here), land_ref.at[group, here], own_sem.at[1 + group])

    def own_out(group):
        return pltpu.make_async_copy(
            land_ref.at[group, here], field_part(out_ref, group, here), own_sem.at[1 + groups + group]
        )

    @pl.loop(1, grid)
    def _(distance):
        pl.semaphore_signal(
            barrier, inc=1, device_id=(layer, beside_me(distance)), device_id_type=pl.DeviceIdType.MESH
        )

    @pl.loop(1, layers)
    def _(distance):
        pl.semaphore_signal(
            barrier, inc=1, device_id=(above_me(distance), here), device_id_type=pl.DeviceIdType.MESH
        )

    for group in range(groups):
        own_in(group).start()
    for target in range(grid):
        kind = kind_ref[layer * points + target // share]
        chosen = jnp.zeros(projector_ref.shape[1:], F32)
        for number in range(kinds):
            chosen = jnp.where(kind == number, projector_ref[number], chosen)
        packed_ref[target, :nproj * per] = chosen
        packed_ref[target, nproj * per:nproj * per + per] = potential_ref[target // share]
    own_side().start()
    vector_ref[...] = now_ref[...]
    previous_ref[...] = old_ref[...]
    pl.semaphore_wait(barrier, grid + layers - 2)

    @pl.loop(1, grid)
    def _(distance):
        side_copy(distance, here).start()

    for group in range(groups):
        @pl.loop(1, grid)
        def _(distance):
            in_copy(group, distance, here).start()

    lane = lax.broadcasted_iota(jnp.int32, (1, lanes), 1)
    real = lane < lanes // 2
    block_of = lax.rem(lane, lanes // 2) // orbs
    orbital_of = lax.rem(lane, orbs)
    sign = jnp.where(real, 1.0, -1.0).astype(F32)

    def turn(value, count):
        if blocks == 1:
            return value
        count = count % blocks
        inside = pltpu.roll(value, count * orbs, 1)
        around = pltpu.roll(value, lanes // 2 + count * orbs, 1)
        return jnp.where(lax.rem(lax.broadcasted_iota(jnp.int32, value.shape, 1), lanes // 2) >= count * orbs, inside, around)

    weight = jnp.where(my_kind == 0, strength_ref[0:1, :], 0.0)
    for number in range(1, kinds):
        weight = weight + jnp.where(my_kind == number, strength_ref[number:number + 1, :], 0.0)
    weight = jnp.broadcast_to(weight * (2.0 * SPACING**2), (nproj, nproj))
    eye = lax.broadcasted_iota(jnp.int32, (nproj, nproj), 0) == lax.broadcasted_iota(jnp.int32, (nproj, nproj), 1)
    weight_ref[...] = jnp.broadcast_to(jnp.sum(jnp.where(eye, weight, 0.0), axis=1, keepdims=True), (nproj, lanes))

    own_side().wait()

    @pl.loop(1, grid)
    def _(distance):
        side_copy(distance, here).wait_send()
        side_copy(distance, beside_me(distance)).wait_recv()

    def prepare(slot, carry):
        for half in range(wide):
            here_lanes = slice(half * lanes, (half + 1) * lanes)
            level = []
            for block in range(blocks):
                x = block * slots + slot
                owner, plane = lax.div(x, mine), lax.rem(x, mine)
                row = half * mine + plane
                beta = side_ref[owner, pl.ds(row, nproj, stride=per), :]
                high, low = halves(beta)
                top = block * 2 * nproj
                fore_ref[slot, top:top + nproj, here_lanes] = high
                fore_ref[slot, top + nproj:top + 2 * nproj, here_lanes] = low
                high, low = high.astype(F32), low.astype(F32)
                tall = jnp.concatenate([high, low, high, low], axis=0)
                back_ref[slot, here_lanes, block * lanes:(block + 1) * lanes] = tall.T.astype(BF16)
                level.append(jnp.broadcast_to(side_ref[owner, pl.ds(nproj * per + row, 1), :], (orbs, lanes)))
            diag_ref[slot, here_lanes, :] = jnp.concatenate(level * 2, axis=0).T * (2.0 * SPACING**2)
        return carry

    lax.fori_loop(0, slots, prepare, 0)

    def keep(term, group, slot, rows, value):
        terms_ref[term, group, slot + 1, rows, :] = value

    def edges(term, group):
        def one(step, carry):
            rows = pl.ds(pl.multiple_of(step * NZ, NZ), NZ)
            terms_ref[term, group, 0, rows, :] = turn(terms_ref[term, group, slots, rows, :], 1)
            terms_ref[term, group, slots + 1, rows, :] = turn(terms_ref[term, group, 1, rows, :], blocks - 1)
            return carry

        lax.fori_loop(0, cells // NZ, one, 0, unroll=4)

    def setup(group):
        def one(slot, carry):
            for half in range(wide):
                pieces = []
                for part in range(2):
                    for block in range(blocks):
                        x = block * slots + slot
                        owner, plane = lax.div(x, mine), lax.rem(x, mine)
                        pieces.append(land_ref[group, owner, part, pl.ds(half * mine + plane, orbs, stride=per), :])
                value = jnp.concatenate(pieces, axis=0).T
                rows = slice(half * lanes, (half + 1) * lanes)
                terms_ref[0, group, slot + 1, rows, :] = value
                high, low = halves(value)
                parts_ref[group, slot, rows, :lanes] = high
                parts_ref[group, slot, rows, lanes:] = low
            return carry

        lax.fori_loop(0, slots, one, 0)
        edges(0, group)

    def finish(group):
        def one(slot, carry):
            for half in range(wide):
                value = terms_ref[0, group, slot + 1, half * lanes:(half + 1) * lanes, :]
                occupied = jnp.where(orbital_of + group * orbs < limit, 1.0, 0.0)
                value = (value * occupied).T
                for part in range(2):
                    for block in range(blocks):
                        x = block * slots + slot
                        owner, plane = lax.div(x, mine), lax.rem(x, mine)
                        top = (part * blocks + block) * orbs
                        land_ref[group, owner, part, pl.ds(half * mine + plane, orbs, stride=per), :] = value[top:top + orbs]
            return carry

        lax.fori_loop(0, slots, one, 0)

    def contract(group):
        total = jnp.zeros((blocks * 2 * nproj, 2 * lanes), F32)
        for slot in range(slots):
            total = total + jnp.dot(fore_ref[slot], parts_ref[group, slot], preferred_element_type=F32)
        total = total[:, :lanes] + total[:, lanes:]
        c = jnp.zeros((nproj, lanes), F32)
        for block in range(blocks):
            top = block * 2 * nproj
            both = total[top:top + nproj] + total[top + nproj:top + 2 * nproj]
            c = c + jnp.where(block_of == block, both, 0.0)
        summed = c
        for count in range(1, blocks):
            summed = summed + turn(c, count)
        summed = summed * weight_ref[...]
        high, low = halves(summed)
        tall = jnp.concatenate([high, high, low, low], axis=0).astype(F32)
        return jnp.concatenate([jnp.where(block_of == block, tall, 0.0) for block in range(blocks)], axis=0).astype(BF16)

    def degree_pass(group, degree, a, last_step, acc):
        scale = TIME_STEP / degree
        right = contract(group)
        swap_scale = sign * (scale / (2.0 * SPACING**2))
        drift_scale = a * (scale / (2.0 * SPACING))
        base = 6.0 + (SPACING * SPACING) * a * a
        source = degree - 1
        final = degree == ORDER
        target = 0 if final else degree

        def one(slot, acc):
            nonlocal_part = jnp.dot(back_ref[slot], right, preferred_element_type=F32)
            for y in range(cells // NZ):
                rows = slice(y * NZ, (y + 1) * NZ)
                up = (y + 1) % (cells // NZ) * NZ
                down = (y - 1) % (cells // NZ) * NZ
                value = terms_ref[source, group, slot + 1, rows, :]
                ahead, behind = pltpu.roll(value, NZ - 1, 0), pltpu.roll(value, 1, 0)
                beside = (ahead + behind) + (
                    terms_ref[source, group, slot + 1, up:up + NZ, :] + terms_ref[source, group, slot + 1, down:down + NZ, :]
                ) + (terms_ref[source, group, slot, rows, :] + terms_ref[source, group, slot + 2, rows, :])
                level = (diag_ref[slot, rows, :] + base) * value - beside + nonlocal_part[rows]
                new = swap_scale * pltpu.roll(level, lanes // 2, 1) - drift_scale * (ahead - behind)
                if final:
                    new = new + value
                    for term in range(source):
                        new = new + terms_ref[term, group, slot + 1, rows, :]
                    flow, density = acc
                    slope = pltpu.roll(new, NZ - 1, 0) - pltpu.roll(new, 1, 0)
                    acc = (flow + new * pltpu.roll(slope, lanes // 2, 1), density + new * new)
                terms_ref[target, group, slot + 1, rows, :] = new
                high, low = halves(new)
                parts_ref[group, slot, rows, :lanes] = high
                parts_ref[group, slot, rows, lanes:] = low
            return acc

        acc = lax.fori_loop(0, slots, one, acc)
        edges(target, group)
        return acc

    def advance_group(step, group, a):
        @pl.when(step == 0)
        def _():
            own_in(group).wait()

            @pl.loop(1, grid)
            def _(distance):
                in_copy(group, distance, here).wait_send()
                in_copy(group, distance, beside_me(distance)).wait_recv()

            setup(group)

        acc = (jnp.zeros((NZ, lanes), F32), jnp.zeros((NZ, lanes), F32))
        for degree in range(1, ORDER + 1):
            acc = degree_pass(group, degree, a, False, acc)
        flow, density = acc
        occupied = jnp.where(orbital_of + group * orbs < limit, 1.0, 0.0)

        @pl.when(step == STEPS - 1)
        def _():
            finish(group)

            @pl.loop(1, grid)
            def _(distance):
                out_copy(group, distance, here).start()

            own_out(group).start()

        return jnp.sum(flow * (sign * (0.5 / SPACING)) * occupied + a * density * occupied)

    flat = (
        lax.broadcasted_iota(jnp.int32, now_ref.shape, 0) * now_ref.shape[1]
        + lax.broadcasted_iota(jnp.int32, now_ref.shape, 1)
    )

    def row_copy(step, distance, owner):
        other = beside_me(distance)
        return remote(
            row_ref.at[step], rows_ref.at[step, owner], row_send.at[step, distance], row_recv.at[step, owner], (layer, other)
        )

    def all_copy(step, distance, owner):
        return remote(
            rows_ref.at[step], all_ref.at[step, owner],
            all_send.at[step, distance], all_recv.at[step, owner], (above_me(distance), here),
        )

    def advance(step, carry):
        a = jnp.sum(jnp.where(flat == my_cell, vector_ref[...], 0.0))
        total = lax.fori_loop(0, groups, lambda group, total: total + advance_group(step, group, a), jnp.float32(0.0))
        row_ref[step] = jnp.full((1, LANES), total * norm, F32)

        @pl.loop(1, grid)
        def _(distance):
            row_copy(step, distance, here).start()

        rows_ref[step, here] = row_ref[step]

        @pl.loop(1, grid)
        def _(distance):
            row_copy(step, distance, here).wait_send()
            row_copy(step, distance, beside_me(distance)).wait_recv()

        @pl.loop(1, layers)
        def _(distance):
            all_copy(step, distance, layer).start()

        all_ref[step, layer] = rows_ref[step]

        @pl.loop(1, layers)
        def _(distance):
            all_copy(step, distance, layer).wait_send()
            all_copy(step, distance, above_me(distance)).wait_recv()

        deposit = jnp.zeros(flat.shape, F32)
        for storey in range(layers):
            for member in range(grid):
                cell = cell_ref[storey * points + member // share]
                deposit = deposit + jnp.where(flat == cell, all_ref[step, storey, member], 0.0)
        present = vector_ref[...]
        vector_ref[...] = macro_update(present, previous_ref[...], deposit, macro)
        previous_ref[...] = present
        return carry

    lax.fori_loop(0, STEPS, advance, 0)
    for group in range(groups):
        own_out(group).wait()

        @pl.loop(1, grid)
        def _(distance):
            out_copy(group, distance, here).wait_send()
            out_copy(group, distance, beside_me(distance)).wait_recv()


def propagate(materials, kinds, owners, strengths, projectors, potential, now, old, field, norm, macro, share, grid, layers, mine, own):
    points, per, lanes = potential.shape
    cells = per // mine * lanes
    planes = grid * mine
    orbs = own // GROUPS
    blocks = lanes // (2 * orbs)
    slots = planes // blocks
    nproj = strengths.shape[1]
    rows = nproj * per
    tall = rows + -(-per // 8) * 8
    vmem = pl.BlockSpec(memory_space=pltpu.VMEM)
    smem = pl.BlockSpec(memory_space=pltpu.SMEM)
    anywhere = pl.BlockSpec(memory_space=pl.ANY)
    dma = lambda *shape: pltpu.SemaphoreType.DMA(shape)
    return pl.pallas_call(
        functools.partial(kernel, norm, macro, share, grid, layers, mine, own),
        out_shape=(
            jax.ShapeDtypeStruct(field.shape, F32),
            jax.ShapeDtypeStruct(now.shape, F32),
        ),
        in_specs=[smem] * 3 + [vmem] * 5 + [anywhere],
        out_specs=(anywhere, vmem),
        scratch_shapes=[
            pltpu.VMEM((ORDER, GROUPS, slots + 2, cells, lanes), F32),
            pltpu.VMEM((GROUPS, grid, 2, orbs * per, lanes), F32),
            pltpu.VMEM((GROUPS, slots, cells, 2 * lanes), BF16),
            pltpu.VMEM((grid, tall, lanes), F32),
            pltpu.VMEM((grid, tall, lanes), F32),
            pltpu.VMEM((slots, blocks * 2 * nproj, cells), BF16),
            pltpu.VMEM((slots, cells, blocks * lanes), BF16),
            pltpu.VMEM((slots, cells, lanes), F32),
            pltpu.VMEM((nproj, lanes), F32),
            pltpu.VMEM(now.shape, F32),
            pltpu.VMEM((STEPS, 1, LANES), F32),
            pltpu.VMEM((STEPS, grid, 1, LANES), F32),
            pltpu.VMEM((STEPS, layers, grid, 1, LANES), F32),
            dma(GROUPS, grid), dma(GROUPS, grid),
            dma(grid), dma(grid),
            dma(GROUPS, grid), dma(GROUPS, grid),
            dma(STEPS, grid), dma(STEPS, grid),
            dma(STEPS, layers), dma(STEPS, layers),
            dma(1 + 2 * GROUPS),
        ],
        compiler_params=pltpu.CompilerParams(
            vmem_limit_bytes=48 * 1024 * 1024, collective_id=0, has_side_effects=True
        ),
        name="propagate",
    )(materials, kinds, owners, strengths, projectors, potential, now, old, field)


def rows_of(array, lanes=LANES):
    lead, (planes, cells) = array.shape[:-2], array.shape[-2:]
    array = array.reshape(lead + (planes, cells // lanes, lanes))
    return jnp.swapaxes(array, -3, -2).reshape(lead + (planes * cells // lanes, lanes))


def local(
    orbitals, local_potential, projectors, strengths, material, proj_kind, point_cell,
    vector_now, vector_old, grid, layers,
):
    _, points, orb, mine, cells = orbitals.shape
    assert grid % points == 0 and orb % (grid // points) == 0
    share = grid // points
    own = orb // share
    wide = cells // LANES
    per = wide * mine
    kinds, nproj = strengths.shape
    macro = vector_now.shape[0]
    padded = (macro // 1024 + 1) * 1024
    lay = lambda vector: jnp.pad(vector, (0, padded - macro)).reshape(-1, LANES)
    field, vector = propagate(
        material, proj_kind, point_cell, strengths,
        rows_of(projectors).reshape(kinds, nproj * per, LANES),
        rows_of(local_potential),
        lay(vector_now), lay(vector_old),
        rows_of(orbitals).reshape(2, points, orb * per, LANES),
        2.0 / (orb * grid * mine * cells), macro, share, grid, layers, mine, own,
    )
    field = jnp.swapaxes(field.reshape(2, points, orb, wide, mine, LANES), -3, -2).reshape(orbitals.shape)
    return field, vector.reshape(-1)[:macro]


def solution(mesh):
    in_specs = (
        P(None, "micro", None, "grid", None),
        P("micro", "grid", None),
        P(None, None, "grid", None),
        P(),
        P(),
        P(),
        P(),
        P(),
        P(),
    )
    out_specs = (P(None, "micro", None, "grid", None), P())
    body = functools.partial(local, grid=mesh.shape["grid"], layers=mesh.shape["micro"])
    return jax.shard_map(body, mesh=mesh, in_specs=in_specs, out_specs=out_specs, check_vma=False)
```

time: 111 us -> 113 us (1.018)
  Pallas kernels: 101 us -> 104 us
  other arithmetic: 1.2 us -> 0 us
    unnamed x11 -> x16, local copies, waits for them, and re-layouts: 1.3 us -> 7.77 us
    pallas_call x1, Pallas kernels: 101 us -> 104 us  [propagate(): pl.pallas_call(functools.partial(kernel, norm, macro, share, grid, layers...]
    reshape x2 -> x1, local copies, waits for them, and re-layouts: 3.68 us -> 0.72 us  [local(): lay = lambda vector: jnp.pad(vector, (0, padded - macro)).reshape(-1, LANES)]
    gather x2 -> x0, local copies, waits for them, and re-layouts: 1.16 us -> none  [local(): jnp.take(projectors, kinds, axis=0, mode='clip').transpose(0, 2, 1, 3)]
where the time goes in v1:
time: 113 us
  Pallas kernels  104 us (92%)
  local copies, waits for them, and re-layouts  8.49 us (8%)
    pallas_call x1, Pallas kernels, propagate(): pl.pallas_call(functools.partial(kernel, norm, macro, share, grid, layers...  104 us
    unnamed x16, local copies, waits for them, and re-layouts  7.77 us

profile of v1, /device:TPU:0, one launch (start us, length us, event | category | flops | bytes accessed | tf_op | source)
XLA Modules:
  0.0 112.9 jit_solution(15859237253214409997)
XLA Ops:
  0.6 0.7 pad_bitcast_fusion
  1.3 0.0 copy-start
  1.4 1.6 %copy-done = f32[2,8,64,2,256]{4,3,2,1,0:T(2,128)S(1)} copy-done((f32[2,8,64,2,256]{4,3,2,1,0:T(2,128)S(1)}, f32[2,8,64,2,256]{4,3,2,1,0:T(2,128)}, u32[]{:S(2)}) %copy-start) | copy-done | bytes 2097176
  2.9 0.0 copy-start.1
  2.9 0.9 copy-done.1
  3.8 0.0 copy-start.2
  3.8 0.7 copy-done.2
  4.6 0.0 copy-start.3
  4.6 0.7 copy-done.3
  5.2 0.0 copy-start.4
  5.2 0.7 copy-done.4
  5.9 0.0 copy-start.5
  5.9 0.7 copy-done.5
  6.6 0.0 copy-start.6
  6.6 0.7 copy-done.6
  7.2 103.7 %propagate.1 = (f32[2,8,256,128]{3,2,1,0:T(8,128)S(1)}, f32[16,128]{1,0:T(8,128)S(1)}) custom-call(s32[32]{0:T(128)S(1)} %copy-done.4, s32[32]{0:T(128)S(1)} %copy-done.5, s32[32]{0:T(128)S(1)} %copy-done.6, f32[2,32]{1,0:T(2,128)S(1)} %copy-done.3, f32[2,128,128]{2,1,0:T(8,128)S(1)} %bitcast.28, f32[8,4,128]{2,1,0:T(4,128)S(1)} %bitcast.29, ...), custom_call_target="tpu_custom_call" | custom-call | tf_op jit(solution)/shard_map/propagate/pallas_call | solution.py:414
  110.9 1.3 %copy.17 = f32[2,8,64,2,256]{4,3,2,1,0:T(2,128)} copy(f32[2,8,64,2,256]{4,3,2,1,0:T(2,128)S(1)} %bitcast.27) | data formatting | bytes 4194304
  112.3 0.6 copy.18
Async XLA Ops:
  1.3 1.6 %copy-start = (f32[2,8,64,2,256]{4,3,2,1,0:T(2,128)S(1)}, f32[2,8,64,2,256]{4,3,2,1,0:T(2,128)}, u32[]{:S(2)}) copy-start(f32[2,8,64,2,256]{4,3,2,1,0:T(2,128)} %param.9) | copy-start | bytes 6291460
  2.9 0.9 copy-start.1
  3.8 0.7 copy-start.2
  4.6 0.7 copy-start.3
  5.2 0.7 copy-start.4
  5.9 0.7 copy-start.5
  6.6 0.7 copy-start.6

commit v2 on v1

v2 whole, which is shorter than its diff:
```python
import functools

import jax
import jax.numpy as jnp
from jax import lax
from jax.experimental import pallas as pl
from jax.experimental.pallas import tpu as pltpu
from jax.sharding import PartitionSpec as P

NZ = 16
STEPS = 2
ORDER = 4
LANES = 128
GROUPS = 4

SPACING = 0.64
TIME_STEP = 0.05
COURANT = 0.9
COUPLING = 1.0
F32 = jnp.float32
BF16 = jnp.bfloat16


def halves(value):
    high = value.astype(BF16)
    return high, (value - high.astype(F32)).astype(BF16)


def macro_update(present, previous, deposit, macro):
    high, lanes = present.shape
    lane = lax.broadcasted_iota(jnp.int32, present.shape, 1)
    flat = lax.broadcasted_iota(jnp.int32, present.shape, 0) * lanes + lane
    ahead = pltpu.roll(present, lanes - 1, 1)
    ahead = jnp.where(lane == lanes - 1, pltpu.roll(ahead, high - 1, 0), ahead)
    behind = pltpu.roll(present, 1, 1)
    behind = jnp.where(lane == 0, pltpu.roll(behind, 1, 0), behind)
    curvature = ahead + behind - 2.0 * present
    following = 2.0 * present - previous + COURANT**2 * curvature - COUPLING * deposit
    return jnp.where(flat < macro, following, 0.0)


def kernel(
    norm, macro, share, grid, layers, mine, own,
    material_in, kind_in, cell_in, strength_in, projector_in, potential_in, field_ref, now_ref, old_ref,
    out_ref, vector_ref,
    material_ref, kind_ref, cell_ref, strength_ref, projector_ref, potential_ref,
    terms_ref, land_ref, parts_ref, total_ref, packed_ref, side_ref, fore_ref, back_ref, diag_ref, level_ref, weight_ref,
    previous_ref, row_ref, rows_ref, flow_ref,
    in_send, in_recv, side_send, side_recv, out_send, out_recv, row_send, row_recv, load_sem,
):
    _, groups, slots, cells, lanes = terms_ref.shape
    slots = slots - 2
    kinds, nproj = strength_ref.shape
    points, per, _ = potential_ref.shape
    wide = cells // lanes
    orbs = own // groups
    blocks = lanes // (2 * orbs)
    here = lax.axis_index("grid")
    layer = lax.axis_index("micro")
    me = layer * points + lax.div(here, share)
    piece = orbs * per
    barrier = pltpu.get_barrier_semaphore()

    loads = [
        pltpu.make_async_copy(source, target, load_sem.at[number])
        for number, (source, target) in enumerate((
            (material_in, material_ref), (kind_in, kind_ref), (cell_in, cell_ref),
            (strength_in, strength_ref), (projector_in, projector_ref), (potential_in, potential_ref),
        ))
    ]

    def partner(mask):
        other, bit = 0, 1
        while bit < grid:
            own_bit = lax.rem(lax.div(here, bit), 2)
            other = other + (1 - own_bit if mask & bit else own_bit) * bit
            bit *= 2
        return other

    partners = {mask: partner(mask) for mask in range(1, grid)}
    core = lax.rem(here, 2)

    def ordered():
        chips = list(range(1, grid // 2))
        swapped = list(chips)
        if len(chips) >= 2:
            swapped[0], swapped[1] = chips[1], chips[0]
        for first, second in zip(chips, swapped):
            for bit in range(2):
                one, two = 2 * first + bit, 2 * second + bit
                yield one, two
        yield 1, 1

    order = []
    for one, two in ordered():
        order.append(partners[one] if one == two else partners[one] + core * (partners[two] - partners[one]))

    def storey(distance):
        return lax.rem(layer + distance, layers)

    def remote(source, target, sent, received, device):
        return pltpu.make_async_remote_copy(
            src_ref=source, dst_ref=target, send_sem=sent, recv_sem=received,
            device_id=device, device_id_type=pl.DeviceIdType.MESH,
        )

    def field_part(ref, group, device):
        first = (lax.rem(device, share) * own + group * orbs) * per
        return ref.at[:, lax.div(device, share), pl.ds(pl.multiple_of(first, 8), piece), :]

    def all_bytes(ref, sem):
        pltpu.make_async_copy(ref, ref, sem).wait()

    def signal(device):
        pl.semaphore_signal(barrier, inc=1, device_id=device, device_id_type=pl.DeviceIdType.MESH)

    for copy in loads:
        copy.start()
    for distance in range(layers):
        if distance > 0:
            signal((storey(distance), here))
        for other in partners.values():
            signal((storey(distance), other))

    def own_in(group):
        return pltpu.make_async_copy(field_part(field_ref, group, here), land_ref.at[group, here], in_recv.at[group])

    def own_out(group):
        return pltpu.make_async_copy(land_ref.at[group, here], field_part(out_ref, group, here), out_recv.at[group])

    def own_side():
        return pltpu.make_async_copy(packed_ref.at[here], side_ref.at[here], side_recv)

    for group in range(groups):
        own_in(group).start()
    for copy in loads:
        copy.wait()
    limit = jnp.where(material_ref[me] == 1, share * own, share * own // 2) - lax.rem(here, share) * own
    my_cell, my_kind = cell_ref[me], kind_ref[me]
    for target in range(grid):
        kind = kind_ref[layer * points + target // share]
        chosen = jnp.zeros(projector_ref.shape[1:], F32)
        for number in range(kinds):
            chosen = jnp.where(kind == number, projector_ref[number], chosen)
        packed_ref[target, :nproj * per] = chosen
        packed_ref[target, nproj * per:nproj * per + per] = potential_ref[target // share]
        spare = packed_ref.shape[1] - nproj * per - per
        if spare:
            packed_ref[target, nproj * per + per:] = jnp.zeros((spare, lanes), F32)
    own_side().start()
    pl.semaphore_wait(barrier, grid * layers - 1)
    for other in order:
        remote(packed_ref.at[other], side_ref.at[here], side_send, side_recv, (layer, other)).start()
    for group in range(groups):
        for other in order:
            remote(
                field_part(field_ref, group, other), land_ref.at[group, here],
                in_send.at[group], in_recv.at[group], (layer, other),
            ).start()

    vector_ref[...] = now_ref[...]
    previous_ref[...] = old_ref[...]
    lane = lax.broadcasted_iota(jnp.int32, (1, lanes), 1)
    block_of = lax.rem(lane, lanes // 2) // orbs
    orbital_of = lax.rem(lane, orbs)
    sign = jnp.where(lane < lanes // 2, 1.0, -1.0).astype(F32)
    place = lax.rem(lax.broadcasted_iota(jnp.int32, (NZ, lanes), 1), lanes // 2)

    def turn(value, count):
        if blocks == 1:
            return value
        shift = count % blocks * orbs
        mask = place[:value.shape[0]] >= shift
        return jnp.where(mask, pltpu.roll(value, shift, 1), pltpu.roll(value, lanes // 2 + shift, 1))

    weight = jnp.where(my_kind == 0, strength_ref[0:1, :], 0.0)
    for number in range(1, kinds):
        weight = weight + jnp.where(my_kind == number, strength_ref[number:number + 1, :], 0.0)
    weight = jnp.broadcast_to(weight * (2.0 * SPACING**2), (nproj, nproj))
    eye = lax.broadcasted_iota(jnp.int32, (nproj, nproj), 0) == lax.broadcasted_iota(jnp.int32, (nproj, nproj), 1)
    weight_ref[...] = jnp.broadcast_to(jnp.sum(jnp.where(eye, weight, 0.0), axis=1, keepdims=True), (nproj, lanes))

    all_bytes(side_ref, side_recv)

    def prepare(slot, carry):
        for half in range(wide):
            here_lanes = slice(half * lanes, (half + 1) * lanes)
            level = []
            for block in range(blocks):
                x = block * slots + slot
                owner, plane = lax.div(x, mine), lax.rem(x, mine)
                row = half * mine + plane
                beta = side_ref[owner, pl.ds(row, nproj, stride=per), :]
                high, low = halves(beta)
                top = block * 2 * nproj
                fore_ref[slot, top:top + nproj, here_lanes] = high
                fore_ref[slot, top + nproj:top + 2 * nproj, here_lanes] = low
                high, low = high.astype(F32), low.astype(F32)
                tall = jnp.concatenate([high, low, high, low], axis=0)
                back_ref[slot, here_lanes, block * lanes:(block + 1) * lanes] = tall.T.astype(BF16)
                level.append(jnp.broadcast_to(side_ref[owner, pl.ds(nproj * per + row, 1), :], (orbs, lanes)))
            diag_ref[slot, here_lanes, :] = jnp.concatenate(level * 2, axis=0).T * (2.0 * SPACING**2)
        return carry

    lax.fori_loop(0, slots, prepare, 0)

    def place_of(block, slot):
        x = block * slots + slot
        return lax.div(x, mine), lax.rem(x, mine)

    def store(term, group, slot, rows, value):
        terms_ref[term, group, slot + 1, rows, :] = value
        if slot == 0:
            terms_ref[term, group, slots + 1, rows, :] = turn(value, blocks - 1)
        if slot == slots - 1:
            terms_ref[term, group, 0, rows, :] = turn(value, 1)

    def setup(group):
        for slot in range(slots):
            for half in range(wide):
                pieces = []
                for part in range(2):
                    for block in range(blocks):
                        owner, plane = divmod(block * slots + slot, mine)
                        pieces.append(land_ref[group, owner, part, pl.ds(half * mine + plane, orbs, stride=per), :])
                value = jnp.concatenate(pieces, axis=0).T
                for y in range(lanes // NZ):
                    top = half * lanes + y * NZ
                    store(0, group, slot, slice(top, top + NZ), value[y * NZ:(y + 1) * NZ])

    def begin(group):
        total = jnp.zeros((blocks * 2 * nproj, 2 * lanes), F32)
        for slot in range(slots):
            high, low = halves(terms_ref[0, group, slot + 1])
            pieces = jnp.concatenate([high, low], axis=1)
            total = total + jnp.dot(fore_ref[slot], pieces, preferred_element_type=F32)
        total_ref[group] = total[:, :lanes] + total[:, lanes:]

    def finish(group):
        occupied = jnp.where(orbital_of + group * orbs < limit, 1.0, 0.0)
        for slot in range(slots):
            for half in range(wide):
                value = terms_ref[0, group, slot + 1, half * lanes:(half + 1) * lanes, :]
                value = (value * occupied).T
                for part in range(2):
                    for block in range(blocks):
                        owner, plane = divmod(block * slots + slot, mine)
                        top = (part * blocks + block) * orbs
                        land_ref[group, owner, part, pl.ds(half * mine + plane, orbs, stride=per), :] = value[top:top + orbs]

    def spread(total):
        c = jnp.zeros((nproj, lanes), F32)
        for block in range(blocks):
            top = block * 2 * nproj
            both = total[top:top + nproj] + total[top + nproj:top + 2 * nproj]
            c = c + jnp.where(block_of == block, both, 0.0)
        summed = c
        for count in range(1, blocks):
            summed = summed + jnp.concatenate([turn(c[:NZ], count), turn(c[NZ:], count)], axis=0)
        summed = summed * weight_ref[...]
        high, low = halves(summed)
        tall = jnp.concatenate([high, high, low, low], axis=0).astype(F32)
        return jnp.concatenate([jnp.where(block_of == block, tall, 0.0) for block in range(blocks)], axis=0).astype(BF16)

    def degrees(group, a):
        flow, density = jnp.zeros((NZ, lanes), F32), jnp.zeros((NZ, lanes), F32)
        total = total_ref[group]
        for degree in range(1, ORDER + 1):
            scale = TIME_STEP / degree
            right = spread(total)
            swap_scale = sign * (scale / (2.0 * SPACING**2))
            drift_scale = a * (scale / (2.0 * SPACING))
            source = degree - 1
            final = degree == ORDER
            for slot in range(slots):
                nonlocal_part = jnp.dot(back_ref[slot], right, preferred_element_type=F32)
                for y in range(cells // NZ):
                    rows = slice(y * NZ, (y + 1) * NZ)
                    up = (y + 1) % (cells // NZ) * NZ
                    down = (y - 1) % (cells // NZ) * NZ
                    value = terms_ref[source, group, slot + 1, rows, :]
                    ahead, behind = pltpu.roll(value, NZ - 1, 0), pltpu.roll(value, 1, 0)
                    beside = (ahead + behind) + (
                        terms_ref[source, group, slot + 1, up:up + NZ, :]
                        + terms_ref[source, group, slot + 1, down:down + NZ, :]
                    ) + (terms_ref[source, group, slot, rows, :] + terms_ref[source, group, slot + 2, rows, :])
                    level = level_ref[slot, rows, :] * value - beside + nonlocal_part[rows]
                    new = swap_scale * pltpu.roll(level, lanes // 2, 1) - drift_scale * (ahead - behind)
                    if final:
                        new = new + value
                        for term in range(source):
                            new = new + terms_ref[term, group, slot + 1, rows, :]
                        slope = pltpu.roll(new, NZ - 1, 0) - pltpu.roll(new, 1, 0)
                        flow = flow + new * pltpu.roll(slope, lanes // 2, 1)
                        density = density + new * new
                        store(0, group, slot, rows, new)
                    else:
                        store(degree, group, slot, rows, new)
                        parts_ref[slot * cells + y * NZ:slot * cells + (y + 1) * NZ, :] = new.astype(BF16)
                if not final:
                    part = jnp.dot(fore_ref[slot], parts_ref[slot * cells:(slot + 1) * cells, :], preferred_element_type=F32)
                    total = part if slot == 0 else total + part
        flow_ref[0] = flow_ref[0] + flow * jnp.where(orbital_of + group * orbs < limit, sign * (0.5 / SPACING), 0.0)
        flow_ref[1] = flow_ref[1] + density * jnp.where(orbital_of + group * orbs < limit, 1.0, 0.0)

    flat = (
        lax.broadcasted_iota(jnp.int32, now_ref.shape, 0) * now_ref.shape[1]
        + lax.broadcasted_iota(jnp.int32, now_ref.shape, 1)
    )

    def advance(step, carry):
        a = jnp.sum(jnp.where(flat == my_cell, vector_ref[...], 0.0))
        base = 6.0 + (SPACING * SPACING) * a * a
        for slot in range(slots):
            level_ref[slot] = diag_ref[slot] + base
        flow_ref[...] = jnp.zeros(flow_ref.shape, F32)

        def advance_group(group, carry):
            @pl.when(step == 0)
            def _():
                all_bytes(land_ref.at[group], in_recv.at[group])
                setup(group)
                begin(group)

            degrees(group, a)

            @pl.when(step == STEPS - 1)
            def _():
                finish(group)
                for other in order:
                    remote(
                        land_ref.at[group, other], field_part(out_ref, group, here),
                        out_send.at[group], out_recv.at[group], (layer, other),
                    ).start()
                own_out(group).start()

            return carry

        lax.fori_loop(0, groups, advance_group, 0)
        row_ref[step] = jnp.full((1, LANES), jnp.sum(flow_ref[0] + a * flow_ref[1]) * norm, F32)
        mine_row = pltpu.make_async_copy(row_ref.at[step], rows_ref.at[step, layer * grid + here], row_recv.at[step])
        mine_row.start()
        for distance in range(layers - 1, -1, -1):
            for mask in range(grid):
                if distance > 0 or mask > 0:
                    other = partners[mask] if mask else here
                    remote(
                        row_ref.at[step], rows_ref.at[step, layer * grid + here],
                        row_send.at[step], row_recv.at[step], (storey(distance), other),
                    ).start()

        @pl.when(step == 0)
        def _():
            def again(group, carry):
                begin(group)
                return carry

            lax.fori_loop(0, groups, again, 0)

        all_bytes(rows_ref.at[step], row_recv.at[step])
        deposit = jnp.zeros(flat.shape, F32)
        for floor in range(layers):
            for member in range(grid):
                cell = cell_ref[floor * points + member // share]
                deposit = deposit + jnp.where(flat == cell, rows_ref[step, floor * grid + member], 0.0)
        present = vector_ref[...]
        vector_ref[...] = macro_update(present, previous_ref[...], deposit, macro)
        previous_ref[...] = present
        return carry

    lax.fori_loop(0, STEPS, advance, 0)
    all_bytes(packed_ref.at[pl.ds(0, grid - 1)], side_send)
    for step in range(STEPS):
        all_bytes(rows_ref.at[step, pl.ds(0, grid * layers - 1)], row_send.at[step])
    for group in range(groups):
        all_bytes(land_ref.at[group, pl.ds(0, grid - 1)], in_send.at[group])
        all_bytes(land_ref.at[group, pl.ds(0, grid - 1)], out_send.at[group])
        all_bytes(land_ref.at[group], out_recv.at[group])


def propagate(materials, kinds, owners, strengths, projectors, potential, field, now, old, norm, macro, share, grid, layers, mine, own):
    points, per, lanes = potential.shape
    cells = per // mine * lanes
    planes = grid * mine
    orbs = own // GROUPS
    blocks = lanes // (2 * orbs)
    slots = planes // blocks
    nproj = strengths.shape[1]
    rows = nproj * per
    tall = rows + -(-per // 8) * 8
    vmem = pl.BlockSpec(memory_space=pltpu.VMEM)
    hbm = pl.BlockSpec(memory_space=pltpu.HBM)
    dma = lambda *shape: pltpu.SemaphoreType.DMA(shape)
    return pl.pallas_call(
        functools.partial(kernel, norm, macro, share, grid, layers, mine, own),
        out_shape=(
            jax.ShapeDtypeStruct(field.shape, F32),
            jax.ShapeDtypeStruct(now.shape, F32),
        ),
        in_specs=[hbm] * 7 + [vmem] * 2,
        out_specs=(hbm, vmem),
        scratch_shapes=[
            pltpu.SMEM(materials.shape, jnp.int32),
            pltpu.SMEM(kinds.shape, jnp.int32),
            pltpu.SMEM(owners.shape, jnp.int32),
            pltpu.VMEM(strengths.shape, F32),
            pltpu.VMEM(projectors.shape, F32),
            pltpu.VMEM(potential.shape, F32),
            pltpu.VMEM((ORDER, GROUPS, slots + 2, cells, lanes), F32),
            pltpu.VMEM((GROUPS, grid, 2, orbs * per, lanes), F32),
            pltpu.VMEM((slots * cells, lanes), BF16),
            pltpu.VMEM((GROUPS, blocks * 2 * nproj, lanes), F32),
            pltpu.VMEM((grid, tall, lanes), F32),
            pltpu.VMEM((grid, tall, lanes), F32),
            pltpu.VMEM((slots, blocks * 2 * nproj, cells), BF16),
            pltpu.VMEM((slots, cells, blocks * lanes), BF16),
            pltpu.VMEM((slots, cells, lanes), F32),
            pltpu.VMEM((slots, cells, lanes), F32),
            pltpu.VMEM((nproj, lanes), F32),
            pltpu.VMEM(now.shape, F32),
            pltpu.VMEM((STEPS, 1, LANES), F32),
            pltpu.VMEM((STEPS, layers * grid, 1, LANES), F32),
            pltpu.VMEM((2, NZ, lanes), F32),
            dma(GROUPS), dma(GROUPS),
            pltpu.SemaphoreType.DMA, pltpu.SemaphoreType.DMA,
            dma(GROUPS), dma(GROUPS),
            dma(STEPS), dma(STEPS),
            dma(6),
        ],
        compiler_params=pltpu.CompilerParams(
            vmem_limit_bytes=48 * 1024 * 1024, collective_id=0, has_side_effects=True
        ),
        name="propagate",
    )(materials, kinds, owners, strengths, projectors, potential, field, now, old)


def rows_of(array, lanes=LANES):
    lead, (planes, cells) = array.shape[:-2], array.shape[-2:]
    array = array.reshape(lead + (planes, cells // lanes, lanes))
    return jnp.swapaxes(array, -3, -2).reshape(lead + (planes * cells // lanes, lanes))


def local(
    orbitals, local_potential, projectors, strengths, material, proj_kind, point_cell,
    vector_now, vector_old, grid, layers,
):
    _, points, orb, mine, cells = orbitals.shape
    assert grid % points == 0 and orb % (grid // points) == 0
    share = grid // points
    own = orb // share
    wide = cells // LANES
    per = wide * mine
    kinds, nproj = strengths.shape
    macro = vector_now.shape[0]
    padded = (macro // 1024 + 1) * 1024
    lay = lambda vector: jnp.pad(vector, (0, padded - macro)).reshape(-1, LANES)
    field, vector = propagate(
        material, proj_kind, point_cell, strengths,
        rows_of(projectors).reshape(kinds, nproj * per, LANES),
        rows_of(local_potential),
        rows_of(orbitals).reshape(2, points, orb * per, LANES),
        lay(vector_now), lay(vector_old),
        2.0 / (orb * grid * mine * cells), macro, share, grid, layers, mine, own,
    )
    field = jnp.swapaxes(field.reshape(2, points, orb, wide, mine, LANES), -3, -2).reshape(orbitals.shape)
    return field, vector.reshape(-1)[:macro]


def solution(mesh):
    in_specs = (
        P(None, "micro", None, "grid", None),
        P("micro", "grid", None),
        P(None, None, "grid", None),
        P(),
        P(),
        P(),
        P(),
        P(),
        P(),
    )
    out_specs = (P(None, "micro", None, "grid", None), P())
    body = functools.partial(local, grid=mesh.shape["grid"], layers=mesh.shape["micro"])
    return jax.shard_map(body, mesh=mesh, in_specs=in_specs, out_specs=out_specs, check_vma=False)
```

time: 113 us -> 86.2 us (0.76)
  Pallas kernels: 104 us -> 76.6 us
    pallas_call x1, Pallas kernels: 104 us -> 76.6 us  [propagate(): pl.pallas_call(functools.partial(kernel, norm, macro, share, grid, layers...]
where the time goes in v2:
time: 86.2 us; the launch traced here: 85.7 us
  Pallas kernels  76.6 us (89%)
  local copies, waits for them, and re-layouts  8.49 us (10%)
    pallas_call x1, Pallas kernels, propagate(): pl.pallas_call(functools.partial(kernel, norm, macro, share, grid, layers...  76.6 us
    unnamed x16, local copies, waits for them, and re-layouts  7.77 us

profile of v2, /device:TPU:0, one launch (start us, length us, event | category | flops | bytes accessed | tf_op | source)
XLA Modules:
  0.0 85.7 jit_solution(9390500112232650666)
XLA Ops:
  0.6 0.7 pad_bitcast_fusion
  1.3 0.0 copy-start
  1.4 1.6 %copy-done = f32[2,8,64,2,256]{4,3,2,1,0:T(2,128)S(1)} copy-done((f32[2,8,64,2,256]{4,3,2,1,0:T(2,128)S(1)}, f32[2,8,64,2,256]{4,3,2,1,0:T(2,128)}, u32[]{:S(2)}) %copy-start) | copy-done | bytes 2097176
  2.9 0.0 copy-start.1
  2.9 0.9 %copy-done.1 = f32[2,32,2,256]{3,2,1,0:T(2,128)S(1)} copy-done((f32[2,32,2,256]{3,2,1,0:T(2,128)S(1)}, f32[2,32,2,256]{3,2,1,0:T(2,128)}, u32[]{:S(2)}) %copy-start.1) | copy-done | bytes 131096
  3.8 0.0 copy-start.2
  3.8 0.7 copy-done.2
  4.6 0.0 copy-start.3
  4.6 0.7 copy-done.3
  5.2 0.0 copy-start.4
  5.2 0.7 copy-done.4
  5.9 0.0 copy-start.5
  5.9 0.7 copy-done.5
  6.6 0.0 copy-start.6
  6.6 0.7 copy-done.6
  7.2 76.6 %propagate.1 = (f32[2,8,256,128]{3,2,1,0:T(8,128)S(1)}, f32[16,128]{1,0:T(8,128)S(1)}) custom-call(s32[32]{0:T(128)S(1)} %copy-done.4, s32[32]{0:T(128)S(1)} %copy-done.5, s32[32]{0:T(128)S(1)} %copy-done.6, f32[2,32]{1,0:T(2,128)S(1)} %copy-done.3, f32[2,128,128]{2,1,0:T(8,128)S(1)} %bitcast.28, f32[8,4,128]{2,1,0:T(4,128)S(1)} %bitcast.29, ...), custom_call_target="tpu_custom_call" | custom-call | tf_op jit(solution)/shard_map/propagate/pallas_call | solution.py:394
  83.8 1.3 %copy.17 = f32[2,8,64,2,256]{4,3,2,1,0:T(2,128)} copy(f32[2,8,64,2,256]{4,3,2,1,0:T(2,128)S(1)} %bitcast.27) | data formatting | bytes 4194304
  85.1 0.6 copy.18
Async XLA Ops:
  1.3 1.6 %copy-start = (f32[2,8,64,2,256]{4,3,2,1,0:T(2,128)S(1)}, f32[2,8,64,2,256]{4,3,2,1,0:T(2,128)}, u32[]{:S(2)}) copy-start(f32[2,8,64,2,256]{4,3,2,1,0:T(2,128)} %param.9) | copy-start | bytes 6291460
  2.9 0.9 %copy-start.1 = (f32[2,32,2,256]{3,2,1,0:T(2,128)S(1)}, f32[2,32,2,256]{3,2,1,0:T(2,128)}, u32[]{:S(2)}) copy-start(f32[2,32,2,256]{3,2,1,0:T(2,128)} %param.11) | copy-start | bytes 393220
  3.8 0.7 copy-start.2
  4.6 0.7 copy-start.3
  5.2 0.7 copy-start.4
  5.9 0.7 copy-start.5
  6.6 0.7 copy-start.6

commit v3 on v2

--- a/solution.py
+++ b/solution.py
@@ -44,12 +44,12 @@
     material_in, kind_in, cell_in, strength_in, projector_in, potential_in, field_ref, now_ref, old_ref,
     out_ref, vector_ref,
     material_ref, kind_ref, cell_ref, strength_ref, projector_ref, potential_ref,
-    terms_ref, land_ref, parts_ref, total_ref, packed_ref, side_ref, fore_ref, back_ref, diag_ref, level_ref, weight_ref,
-    previous_ref, row_ref, rows_ref, flow_ref,
+    first_ref, second_ref, third_ref, fourth_ref, keep_ref, land_ref, parts_ref, total_ref, packed_ref, side_ref, fore_ref, back_ref, diag_ref, level_ref, weight_ref,
+    previous_ref, row_ref, rows_ref, flow_ref, spare_ref, turned_ref, nonlocal_ref,
     in_send, in_recv, side_send, side_recv, out_send, out_recv, row_send, row_recv, load_sem,
 ):
-    _, groups, slots, cells, lanes = terms_ref.shape
-    slots = slots - 2
+    groups, slots, cells, lanes = keep_ref.shape
+    terms = (first_ref, second_ref, third_ref, fourth_ref)
     kinds, nproj = strength_ref.shape
     points, per, _ = potential_ref.shape
     wide = cells // lanes
@@ -59,6 +59,7 @@
     layer = lax.axis_index("micro")
     me = layer * points + lax.div(here, share)
     piece = orbs * per
+    width = blocks * nproj
     barrier = pltpu.get_barrier_semaphore()
 
     loads = [
@@ -164,14 +165,13 @@
     block_of = lax.rem(lane, lanes // 2) // orbs
     orbital_of = lax.rem(lane, orbs)
     sign = jnp.where(lane < lanes // 2, 1.0, -1.0).astype(F32)
-    place = lax.rem(lax.broadcasted_iota(jnp.int32, (NZ, lanes), 1), lanes // 2)
+    place = lax.rem(lane, lanes // 2)
 
     def turn(value, count):
         if blocks == 1:
             return value
         shift = count % blocks * orbs
-        mask = place[:value.shape[0]] >= shift
-        return jnp.where(mask, pltpu.roll(value, shift, 1), pltpu.roll(value, lanes // 2 + shift, 1))
+        return jnp.where(place >= shift, pltpu.roll(value, shift, 1), pltpu.roll(value, lanes // 2 + shift, 1))
 
     weight = jnp.where(my_kind == 0, strength_ref[0:1, :], 0.0)
     for number in range(1, kinds):
@@ -182,38 +182,51 @@
 
     all_bytes(side_ref, side_recv)
 
+    def parted(ref, top):
+        return ref[pl.ds(top, NZ // 2, stride=2), :], ref[pl.ds(top + 1, NZ // 2, stride=2), :]
+
+    def columns(rows, spare):
+        tall = rows.T
+        for part in range(tall.shape[1] // lanes):
+            spare[part] = tall[:, part * lanes:(part + 1) * lanes]
+        return jnp.concatenate(
+            [
+                jnp.concatenate(
+                    [piece for y in range(lanes // NZ) for piece in parted(spare.at[part], y * NZ)], axis=0
+                )
+                for part in range(tall.shape[1] // lanes)
+            ],
+            axis=1,
+        )
+
     def prepare(slot, carry):
         for half in range(wide):
-            here_lanes = slice(half * lanes, (half + 1) * lanes)
-            level = []
+            level, highs, lows = [], [], []
             for block in range(blocks):
                 x = block * slots + slot
                 owner, plane = lax.div(x, mine), lax.rem(x, mine)
                 row = half * mine + plane
-                beta = side_ref[owner, pl.ds(row, nproj, stride=per), :]
-                high, low = halves(beta)
-                top = block * 2 * nproj
-                fore_ref[slot, top:top + nproj, here_lanes] = high
-                fore_ref[slot, top + nproj:top + 2 * nproj, here_lanes] = low
-                high, low = high.astype(F32), low.astype(F32)
-                tall = jnp.concatenate([high, low, high, low], axis=0)
-                back_ref[slot, here_lanes, block * lanes:(block + 1) * lanes] = tall.T.astype(BF16)
+                high, low = halves(side_ref[owner, pl.ds(row, nproj, stride=per), :])
+                highs.append(high.astype(F32))
+                lows.append(low.astype(F32))
                 level.append(jnp.broadcast_to(side_ref[owner, pl.ds(nproj * per + row, 1), :], (orbs, lanes)))
-            diag_ref[slot, here_lanes, :] = jnp.concatenate(level * 2, axis=0).T * (2.0 * SPACING**2)
+            cells_here = pl.ds(pl.multiple_of(slot * cells + half * lanes, lanes), lanes)
+            for number, part in enumerate((highs, lows)):
+                tall = columns(jnp.concatenate(part, axis=0), spare_ref.at[number])
+                fore_ref[number * width:(number + 1) * width, cells_here] = tall.T.astype(BF16)
+                tall = tall.astype(BF16)
+                back_ref[cells_here, number * width:(number + 1) * width] = tall
+            diag_ref[cells_here, :] = columns(jnp.concatenate(level * 2, axis=0), spare_ref.at[2]) * (2.0 * SPACING**2)
         return carry
 
     lax.fori_loop(0, slots, prepare, 0)
 
-    def place_of(block, slot):
-        x = block * slots + slot
-        return lax.div(x, mine), lax.rem(x, mine)
-
-    def store(term, group, slot, rows, value):
-        terms_ref[term, group, slot + 1, rows, :] = value
+    def store(term, slot, rows, value):
+        terms[term][slot + 1, rows, :] = value
         if slot == 0:
-            terms_ref[term, group, slots + 1, rows, :] = turn(value, blocks - 1)
+            terms[term][slots + 1, rows, :] = turn(value, blocks - 1)
         if slot == slots - 1:
-            terms_ref[term, group, 0, rows, :] = turn(value, 1)
+            terms[term][0, rows, :] = turn(value, 1)
 
     def setup(group):
         for slot in range(slots):
@@ -223,25 +236,39 @@
                     for block in range(blocks):
                         owner, plane = divmod(block * slots + slot, mine)
                         pieces.append(land_ref[group, owner, part, pl.ds(half * mine + plane, orbs, stride=per), :])
-                value = jnp.concatenate(pieces, axis=0).T
+                spare = turned_ref.at[slot * wide + half]
+                spare[...] = jnp.concatenate(pieces, axis=0).T
                 for y in range(lanes // NZ):
                     top = half * lanes + y * NZ
-                    store(0, group, slot, slice(top, top + NZ), value[y * NZ:(y + 1) * NZ])
-
-    def begin(group):
-        total = jnp.zeros((blocks * 2 * nproj, 2 * lanes), F32)
+                    for number, piece in enumerate(parted(spare, y * NZ)):
+                        store(0, slot, slice(top + number * 8, top + number * 8 + 8), piece)
+
+    def begin(group, planes_of):
+        total = jnp.zeros((2 * width, 2 * lanes), F32)
         for slot in range(slots):
-            high, low = halves(terms_ref[0, group, slot + 1])
+            high, low = halves(planes_of(slot))
             pieces = jnp.concatenate([high, low], axis=1)
-            total = total + jnp.dot(fore_ref[slot], pieces, preferred_element_type=F32)
-        total_ref[group] = total[:, :lanes] + total[:, lanes:]
+            total = total + jnp.dot(fore_ref[:, slot * cells:(slot + 1) * cells], pieces, preferred_element_type=F32)
+        total = total[:, :lanes] + total[:, lanes:]
+        total_ref[group] = total[:width] + total[width:]
+
+    def restore(group):
+        for slot in range(slots):
+            for top in range(0, cells, NZ):
+                store(0, slot, slice(top, top + NZ), keep_ref[group, slot, top:top + NZ, :])
 
     def finish(group):
         occupied = jnp.where(orbital_of + group * orbs < limit, 1.0, 0.0)
         for slot in range(slots):
             for half in range(wide):
-                value = terms_ref[0, group, slot + 1, half * lanes:(half + 1) * lanes, :]
-                value = (value * occupied).T
+                spare = turned_ref.at[slot * wide + half]
+                for y in range(lanes // NZ):
+                    top = half * lanes + y * NZ
+                    for number in range(2):
+                        spare[pl.ds(y * NZ + number, 8, stride=2), :] = (
+                            keep_ref[group, slot, top + number * 8:top + number * 8 + 8, :] * occupied
+                        )
+                value = spare[...].T
                 for part in range(2):
                     for block in range(blocks):
                         owner, plane = divmod(block * slots + slot, mine)
@@ -251,55 +278,64 @@
     def spread(total):
         c = jnp.zeros((nproj, lanes), F32)
         for block in range(blocks):
-            top = block * 2 * nproj
-            both = total[top:top + nproj] + total[top + nproj:top + 2 * nproj]
-            c = c + jnp.where(block_of == block, both, 0.0)
+            c = c + jnp.where(block_of == block, total[block * nproj:(block + 1) * nproj], 0.0)
         summed = c
         for count in range(1, blocks):
-            summed = summed + jnp.concatenate([turn(c[:NZ], count), turn(c[NZ:], count)], axis=0)
+            summed = summed + turn(c, count)
         summed = summed * weight_ref[...]
-        high, low = halves(summed)
-        tall = jnp.concatenate([high, high, low, low], axis=0).astype(F32)
-        return jnp.concatenate([jnp.where(block_of == block, tall, 0.0) for block in range(blocks)], axis=0).astype(BF16)
+        high, low = halves(jnp.concatenate([jnp.where(block_of == block, summed, 0.0) for block in range(blocks)], axis=0))
+        both = jnp.concatenate([high, low], axis=1)
+        return jnp.concatenate([both, both], axis=0)
 
     def degrees(group, a):
-        flow, density = jnp.zeros((NZ, lanes), F32), jnp.zeros((NZ, lanes), F32)
+        flow, density = jnp.zeros((8, lanes), F32), jnp.zeros((8, lanes), F32)
         total = total_ref[group]
+        lines = cells // NZ
         for degree in range(1, ORDER + 1):
             scale = TIME_STEP / degree
-            right = spread(total)
             swap_scale = sign * (scale / (2.0 * SPACING**2))
             drift_scale = a * (scale / (2.0 * SPACING))
-            source = degree - 1
+            source = terms[degree - 1]
             final = degree == ORDER
+            both = jnp.dot(back_ref[...], spread(total), preferred_element_type=F32)
+            nonlocal_ref[degree - 1] = both[:, :lanes] + both[:, lanes:]
             for slot in range(slots):
-                nonlocal_part = jnp.dot(back_ref[slot], right, preferred_element_type=F32)
-                for y in range(cells // NZ):
-                    rows = slice(y * NZ, (y + 1) * NZ)
-                    up = (y + 1) % (cells // NZ) * NZ
-                    down = (y - 1) % (cells // NZ) * NZ
-                    value = terms_ref[source, group, slot + 1, rows, :]
-                    ahead, behind = pltpu.roll(value, NZ - 1, 0), pltpu.roll(value, 1, 0)
-                    beside = (ahead + behind) + (
-                        terms_ref[source, group, slot + 1, up:up + NZ, :]
-                        + terms_ref[source, group, slot + 1, down:down + NZ, :]
-                    ) + (terms_ref[source, group, slot, rows, :] + terms_ref[source, group, slot + 2, rows, :])
-                    level = level_ref[slot, rows, :] * value - beside + nonlocal_part[rows]
-                    new = swap_scale * pltpu.roll(level, lanes // 2, 1) - drift_scale * (ahead - behind)
+                for y in range(lines):
+                    tops = (y * NZ, y * NZ + 8)
+                    up, down = (y + 1) % lines * NZ, (y - 1) % lines * NZ
+                    even, odd = (source[slot + 1, top:top + 8, :] for top in tops)
+                    after, before = pltpu.roll(even, 7, 0), pltpu.roll(odd, 1, 0)
+                    fresh = []
+                    for number, (value, ahead, behind) in enumerate(((even, odd, before), (odd, after, even))):
+                        rows = slice(tops[number], tops[number] + 8)
+                        beside = (ahead + behind) + (
+                            source[slot + 1, up + number * 8:up + number * 8 + 8, :]
+                            + source[slot + 1, down + number * 8:down + number * 8 + 8, :]
+                        ) + (source[slot, rows, :] + source[slot + 2, rows, :])
+                        flat_rows = slice(slot * cells + rows.start, slot * cells + rows.stop)
+                        level = level_ref[flat_rows, :] * value - beside + nonlocal_ref[degree - 1, flat_rows, :]
+                        new = swap_scale * pltpu.roll(level, lanes // 2, 1) - drift_scale * (ahead - behind)
+                        if final:
+                            new = new + value
+                            for term in terms[:ORDER - 1]:
+                                new = new + term[slot + 1, rows, :]
+                            keep_ref[group, slot, rows, :] = new
+                        else:
+                            store(degree, slot, rows, new)
+                        fresh.append(new)
                     if final:
-                        new = new + value
-                        for term in range(source):
-                            new = new + terms_ref[term, group, slot + 1, rows, :]
-                        slope = pltpu.roll(new, NZ - 1, 0) - pltpu.roll(new, 1, 0)
-                        flow = flow + new * pltpu.roll(slope, lanes // 2, 1)
-                        density = density + new * new
-                        store(0, group, slot, rows, new)
+                        even, odd = fresh
+                        for value, slope in ((even, odd - pltpu.roll(odd, 1, 0)), (odd, pltpu.roll(even, 7, 0) - even)):
+                            flow = flow + value * pltpu.roll(slope, lanes // 2, 1)
+                            density = density + value * value
                     else:
-                        store(degree, group, slot, rows, new)
-                        parts_ref[slot * cells + y * NZ:slot * cells + (y + 1) * NZ, :] = new.astype(BF16)
-                if not final:
-                    part = jnp.dot(fore_ref[slot], parts_ref[slot * cells:(slot + 1) * cells, :], preferred_element_type=F32)
-                    total = part if slot == 0 else total + part
+                        top = slot * cells + y * NZ
+                        parts_ref[degree - 1, top:top + NZ, :] = jnp.concatenate(fresh, axis=0).astype(BF16)
+                last = slots * cells - cells
+                if not final and slot == slots - 2:
+                    total = jnp.dot(fore_ref[:width, :last], parts_ref[degree - 1, :last, :], preferred_element_type=F32)
+                if not final and slot == slots - 1:
+                    total = total + jnp.dot(fore_ref[:width, last:], parts_ref[degree - 1, last:, :], preferred_element_type=F32)
         flow_ref[0] = flow_ref[0] + flow * jnp.where(orbital_of + group * orbs < limit, sign * (0.5 / SPACING), 0.0)
         flow_ref[1] = flow_ref[1] + density * jnp.where(orbital_of + group * orbs < limit, 1.0, 0.0)
 
@@ -311,8 +347,7 @@
     def advance(step, carry):
         a = jnp.sum(jnp.where(flat == my_cell, vector_ref[...], 0.0))
         base = 6.0 + (SPACING * SPACING) * a * a
-        for slot in range(slots):
-            level_ref[slot] = diag_ref[slot] + base
+        level_ref[...] = diag_ref[...] + base
         flow_ref[...] = jnp.zeros(flow_ref.shape, F32)
 
         def advance_group(group, carry):
@@ -320,7 +355,11 @@
             def _():
                 all_bytes(land_ref.at[group], in_recv.at[group])
                 setup(group)
-                begin(group)
+                begin(group, lambda slot: first_ref[slot + 1])
+
+            @pl.when(step > 0)
+            def _():
+                restore(group)
 
             degrees(group, a)
 
@@ -352,7 +391,7 @@
         @pl.when(step == 0)
         def _():
             def again(group, carry):
-                begin(group)
+                begin(group, lambda slot: keep_ref[group, slot])
                 return carry
 
             lax.fori_loop(0, groups, again, 0)
@@ -406,21 +445,25 @@
             pltpu.VMEM(strengths.shape, F32),
             pltpu.VMEM(projectors.shape, F32),
             pltpu.VMEM(potential.shape, F32),
-            pltpu.VMEM((ORDER, GROUPS, slots + 2, cells, lanes), F32),
+            *[pltpu.VMEM((slots + 2, cells, lanes), F32)] * ORDER,
+            pltpu.VMEM((GROUPS, slots, cells, lanes), F32),
             pltpu.VMEM((GROUPS, grid, 2, orbs * per, lanes), F32),
-            pltpu.VMEM((slots * cells, lanes), BF16),
-            pltpu.VMEM((GROUPS, blocks * 2 * nproj, lanes), F32),
+            pltpu.VMEM((ORDER - 1, slots * cells, lanes), BF16),
+            pltpu.VMEM((GROUPS, blocks * nproj, lanes), F32),
             pltpu.VMEM((grid, tall, lanes), F32),
             pltpu.VMEM((grid, tall, lanes), F32),
-            pltpu.VMEM((slots, blocks * 2 * nproj, cells), BF16),
-            pltpu.VMEM((slots, cells, blocks * lanes), BF16),
-            pltpu.VMEM((slots, cells, lanes), F32),
-            pltpu.VMEM((slots, cells, lanes), F32),
+            pltpu.VMEM((2 * blocks * nproj, slots * cells), BF16),
+            pltpu.VMEM((slots * cells, 2 * blocks * nproj), BF16),
+            pltpu.VMEM((slots * cells, lanes), F32),
+            pltpu.VMEM((slots * cells, lanes), F32),
             pltpu.VMEM((nproj, lanes), F32),
             pltpu.VMEM(now.shape, F32),
             pltpu.VMEM((STEPS, 1, LANES), F32),
             pltpu.VMEM((STEPS, layers * grid, 1, LANES), F32),
-            pltpu.VMEM((2, NZ, lanes), F32),
+            pltpu.VMEM((2, 8, lanes), F32),
+            pltpu.VMEM((3, blocks * nproj // lanes, lanes, lanes), F32),
+            pltpu.VMEM((planes // blocks * (cells // lanes), lanes, lanes), F32),
+            pltpu.VMEM((ORDER, slots * cells, lanes), F32),
             dma(GROUPS), dma(GROUPS),
             pltpu.SemaphoreType.DMA, pltpu.SemaphoreType.DMA,
             dma(GROUPS), dma(GROUPS),
@@ -454,11 +497,12 @@
     macro = vector_now.shape[0]
     padded = (macro // 1024 + 1) * 1024
     lay = lambda vector: jnp.pad(vector, (0, padded - macro)).reshape(-1, LANES)
+    held = lambda array: pltpu.with_memory_space_constraint(array, pltpu.HBM)
     field, vector = propagate(
-        material, proj_kind, point_cell, strengths,
-        rows_of(projectors).reshape(kinds, nproj * per, LANES),
-        rows_of(local_potential),
-        rows_of(orbitals).reshape(2, points, orb * per, LANES),
+        held(material), held(proj_kind), held(point_cell), held(strengths),
+        held(rows_of(projectors).reshape(kinds, nproj * per, LANES)),
+        held(rows_of(local_potential)),
+        held(rows_of(orbitals).reshape(2, points, orb * per, LANES)),
         lay(vector_now), lay(vector_old),
         2.0 / (orb * grid * mine * cells), macro, share, grid, layers, mine, own,
     )

time: 86.2 us -> 76.8 us (0.89)
  local copies, waits for them, and re-layouts: 8.49 us -> 2.64 us
  Pallas kernels: 76.6 us -> 73.2 us
    unnamed x16 -> x2, local copies, waits for them, and re-layouts: 7.77 us -> 1.92 us
    pallas_call x1, Pallas kernels: 76.6 us -> 73.2 us  [propagate(): pl.pallas_call(functools.partial(kernel, norm, macro, share, grid, layers...]
where the time goes in v3:
time: 76.8 us; the launch traced here: 76.5 us
  Pallas kernels  73.2 us (95%)
  local copies, waits for them, and re-layouts  2.64 us (3%)
    pallas_call x1, Pallas kernels, propagate(): pl.pallas_call(functools.partial(kernel, norm, macro, share, grid, layers...  73.2 us
    unnamed x2, local copies, waits for them, and re-layouts  1.92 us

profile of v3, /device:TPU:0, one launch (start us, length us, event | category | flops | bytes accessed | tf_op | source)
XLA Modules:
  0.0 76.5 jit_solution(13713287912508702545)
XLA Ops:
  0.6 0.7 pad_bitcast_fusion
  1.3 73.2 %propagate.1 = (f32[2,8,256,128]{3,2,1,0:T(8,128)S(1)}, f32[16,128]{1,0:T(8,128)S(1)}) custom-call(s32[32]{0:T(128)} %material_in.1, s32[32]{0:T(128)} %kind_in.1, s32[32]{0:T(128)} %cell_in.1, f32[2,32]{1,0:T(2,128)} %strength_in.1, f32[2,128,128]{2,1,0:T(8,128)} %bitcast.29, f32[8,4,128]{2,1,0:T(4,128)} %bitcast.30, f32[2,8,256,128]{3,2,1,0:T(8,128)} %bitcast.28, ...), custom_call_target="tpu_custom_call" | custom-call | tf_op jit(solution)/shard_map/propagate/pallas_call | solution.py:433
  74.6 1.3 %copy.17 = f32[2,8,64,2,256]{4,3,2,1,0:T(2,128)} copy(f32[2,8,64,2,256]{4,3,2,1,0:T(2,128)S(1)} %bitcast.26) | data formatting | bytes 4194304
  75.9 0.6 copy.18

commit v4 on v3

--- a/solution.py
+++ b/solution.py
@@ -26,7 +26,7 @@
     return high, (value - high.astype(F32)).astype(BF16)
 
 
-def macro_update(present, previous, deposit, macro):
+def macro_update(present, previous, macro):
     high, lanes = present.shape
     lane = lax.broadcasted_iota(jnp.int32, present.shape, 1)
     flat = lax.broadcasted_iota(jnp.int32, present.shape, 0) * lanes + lane
@@ -35,18 +35,18 @@
     behind = pltpu.roll(present, 1, 1)
     behind = jnp.where(lane == 0, pltpu.roll(behind, 1, 0), behind)
     curvature = ahead + behind - 2.0 * present
-    following = 2.0 * present - previous + COURANT**2 * curvature - COUPLING * deposit
+    following = 2.0 * present - previous + COURANT**2 * curvature
     return jnp.where(flat < macro, following, 0.0)
 
 
 def kernel(
     norm, macro, share, grid, layers, mine, own,
-    material_in, kind_in, cell_in, strength_in, projector_in, potential_in, field_ref, now_ref, old_ref,
+    material_in, kind_in, cell_in, strength_in, projector_in, potential_in, field_ref, now_in, old_in,
     out_ref, vector_ref,
     material_ref, kind_ref, cell_ref, strength_ref, projector_ref, potential_ref,
-    first_ref, second_ref, third_ref, fourth_ref, keep_ref, land_ref, parts_ref, total_ref, packed_ref, side_ref, fore_ref, back_ref, diag_ref, level_ref, weight_ref,
-    previous_ref, row_ref, rows_ref, flow_ref, spare_ref, turned_ref, nonlocal_ref,
-    in_send, in_recv, side_send, side_recv, out_send, out_recv, row_send, row_recv, load_sem,
+    first_ref, second_ref, third_ref, fourth_ref, keep_ref, land_ref, parts_ref, start_ref, packed_ref, side_ref, fore_ref, back_ref, diag_ref, level_ref, weight_ref,
+    previous_ref, line_now_ref, line_old_ref, row_ref, rows_ref, flow_ref, spare_ref, turned_ref, nonlocal_ref, mask_ref,
+    in_send, in_recv, side_send, side_recv, out_send, out_recv, row_send, row_recv, load_sem, ready_sem,
 ):
     groups, slots, cells, lanes = keep_ref.shape
     terms = (first_ref, second_ref, third_ref, fourth_ref)
@@ -67,6 +67,7 @@
         for number, (source, target) in enumerate((
             (material_in, material_ref), (kind_in, kind_ref), (cell_in, cell_ref),
             (strength_in, strength_ref), (projector_in, projector_ref), (potential_in, potential_ref),
+            (now_in, line_now_ref), (old_in, line_old_ref),
         ))
     ]
 
@@ -112,16 +113,15 @@
     def all_bytes(ref, sem):
         pltpu.make_async_copy(ref, ref, sem).wait()
 
-    def signal(device):
-        pl.semaphore_signal(barrier, inc=1, device_id=device, device_id_type=pl.DeviceIdType.MESH)
+    def signal(semaphore, device):
+        pl.semaphore_signal(semaphore, inc=1, device_id=device, device_id_type=pl.DeviceIdType.MESH)
 
     for copy in loads:
         copy.start()
-    for distance in range(layers):
-        if distance > 0:
-            signal((storey(distance), here))
-        for other in partners.values():
-            signal((storey(distance), other))
+    for distance in range(1, layers):
+        signal(barrier, (storey(distance), here))
+    for other in partners.values():
+        signal(barrier, (layer, other))
 
     def own_in(group):
         return pltpu.make_async_copy(field_part(field_ref, group, here), land_ref.at[group, here], in_recv.at[group])
@@ -149,7 +149,7 @@
         if spare:
             packed_ref[target, nproj * per + per:] = jnp.zeros((spare, lanes), F32)
     own_side().start()
-    pl.semaphore_wait(barrier, grid * layers - 1)
+    pl.semaphore_wait(barrier, grid + layers - 2)
     for other in order:
         remote(packed_ref.at[other], side_ref.at[here], side_send, side_recv, (layer, other)).start()
     for group in range(groups):
@@ -159,8 +159,13 @@
                 in_send.at[group], in_recv.at[group], (layer, other),
             ).start()
 
-    vector_ref[...] = now_ref[...]
-    previous_ref[...] = old_ref[...]
+    for distance in range(1, layers):
+        signal(ready_sem, (storey(distance), here))
+    for line, rows in ((line_now_ref, vector_ref), (line_old_ref, previous_ref)):
+        rows[...] = jnp.zeros(rows.shape, F32)
+        for top in range(0, macro, LANES):
+            length = min(LANES, macro - top)
+            rows[top // LANES, :length] = line[pl.ds(top, length)]
     lane = lax.broadcasted_iota(jnp.int32, (1, lanes), 1)
     block_of = lax.rem(lane, lanes // 2) // orbs
     orbital_of = lax.rem(lane, orbs)
@@ -250,7 +255,11 @@
             pieces = jnp.concatenate([high, low], axis=1)
             total = total + jnp.dot(fore_ref[:, slot * cells:(slot + 1) * cells], pieces, preferred_element_type=F32)
         total = total[:, :lanes] + total[:, lanes:]
-        total_ref[group] = total[:width] + total[width:]
+        start_ref[group] = distant(total[:width] + total[width:])
+
+    def distant(total):
+        both = jnp.dot(back_ref[...], spread(total), preferred_element_type=F32)
+        return both[:, :lanes] + both[:, lanes:]
 
     def restore(group):
         for slot in range(slots):
@@ -289,7 +298,7 @@
 
     def degrees(group, a):
         flow, density = jnp.zeros((8, lanes), F32), jnp.zeros((8, lanes), F32)
-        total = total_ref[group]
+        total = None
         lines = cells // NZ
         for degree in range(1, ORDER + 1):
             scale = TIME_STEP / degree
@@ -297,8 +306,9 @@
             drift_scale = a * (scale / (2.0 * SPACING))
             source = terms[degree - 1]
             final = degree == ORDER
-            both = jnp.dot(back_ref[...], spread(total), preferred_element_type=F32)
-            nonlocal_ref[degree - 1] = both[:, :lanes] + both[:, lanes:]
+            if degree > 1:
+                nonlocal_ref[degree - 2] = distant(total)
+            far = start_ref.at[group] if degree == 1 else nonlocal_ref.at[degree - 2]
             for slot in range(slots):
                 for y in range(lines):
                     tops = (y * NZ, y * NZ + 8)
@@ -313,7 +323,7 @@
                             + source[slot + 1, down + number * 8:down + number * 8 + 8, :]
                         ) + (source[slot, rows, :] + source[slot + 2, rows, :])
                         flat_rows = slice(slot * cells + rows.start, slot * cells + rows.stop)
-                        level = level_ref[flat_rows, :] * value - beside + nonlocal_ref[degree - 1, flat_rows, :]
+                        level = level_ref[flat_rows, :] * value - beside + far[flat_rows, :]
                         new = swap_scale * pltpu.roll(level, lanes // 2, 1) - drift_scale * (ahead - behind)
                         if final:
                             new = new + value
@@ -340,12 +350,11 @@
         flow_ref[1] = flow_ref[1] + density * jnp.where(orbital_of + group * orbs < limit, 1.0, 0.0)
 
     flat = (
-        lax.broadcasted_iota(jnp.int32, now_ref.shape, 0) * now_ref.shape[1]
-        + lax.broadcasted_iota(jnp.int32, now_ref.shape, 1)
+        lax.broadcasted_iota(jnp.int32, vector_ref.shape, 0) * vector_ref.shape[1]
+        + lax.broadcasted_iota(jnp.int32, vector_ref.shape, 1)
     )
 
-    def advance(step, carry):
-        a = jnp.sum(jnp.where(flat == my_cell, vector_ref[...], 0.0))
+    def advance(step, a):
         base = 6.0 + (SPACING * SPACING) * a * a
         level_ref[...] = diag_ref[...] + base
         flow_ref[...] = jnp.zeros(flow_ref.shape, F32)
@@ -357,7 +366,7 @@
                 setup(group)
                 begin(group, lambda slot: first_ref[slot + 1])
 
-            @pl.when(step > 0)
+            @pl.when(step * group > 0)
             def _():
                 restore(group)
 
@@ -379,6 +388,11 @@
         row_ref[step] = jnp.full((1, LANES), jnp.sum(flow_ref[0] + a * flow_ref[1]) * norm, F32)
         mine_row = pltpu.make_async_copy(row_ref.at[step], rows_ref.at[step, layer * grid + here], row_recv.at[step])
         mine_row.start()
+
+        @pl.when(step == 0)
+        def _():
+            pl.semaphore_wait(ready_sem, layers - 1)
+
         for distance in range(layers - 1, -1, -1):
             for mask in range(grid):
                 if distance > 0 or mask > 0:
@@ -395,19 +409,27 @@
                 return carry
 
             lax.fori_loop(0, groups, again, 0)
-
+            restore(0)
+
+        present = vector_ref[...]
+        following = macro_update(present, previous_ref[...], macro)
+        own_following = jnp.sum(jnp.where(flat == my_cell, following, 0.0))
+        for floor in range(layers):
+            for member in range(grid):
+                same = cell_ref[floor * points + member // share] == my_cell
+                mask_ref[floor * grid + member] = jnp.full((1, LANES), jnp.where(same, COUPLING / LANES, 0.0), F32)
         all_bytes(rows_ref.at[step], row_recv.at[step])
+        own_deposit = jnp.sum(rows_ref[step] * mask_ref[...])
         deposit = jnp.zeros(flat.shape, F32)
         for floor in range(layers):
             for member in range(grid):
                 cell = cell_ref[floor * points + member // share]
                 deposit = deposit + jnp.where(flat == cell, rows_ref[step, floor * grid + member], 0.0)
-        present = vector_ref[...]
-        vector_ref[...] = macro_update(present, previous_ref[...], deposit, macro)
+        vector_ref[...] = following - COUPLING * deposit
         previous_ref[...] = present
-        return carry
-
-    lax.fori_loop(0, STEPS, advance, 0)
+        return own_following - own_deposit
+
+    lax.fori_loop(0, STEPS, advance, jnp.sum(jnp.where(flat == my_cell, vector_ref[...], 0.0)))
     all_bytes(packed_ref.at[pl.ds(0, grid - 1)], side_send)
     for step in range(STEPS):
         all_bytes(rows_ref.at[step, pl.ds(0, grid * layers - 1)], row_send.at[step])
@@ -434,9 +456,9 @@
         functools.partial(kernel, norm, macro, share, grid, layers, mine, own),
         out_shape=(
             jax.ShapeDtypeStruct(field.shape, F32),
-            jax.ShapeDtypeStruct(now.shape, F32),
+            jax.ShapeDtypeStruct((-(-macro // 1024) * 8, LANES), F32),
         ),
-        in_specs=[hbm] * 7 + [vmem] * 2,
+        in_specs=[hbm] * 9,
         out_specs=(hbm, vmem),
         scratch_shapes=[
             pltpu.SMEM(materials.shape, jnp.int32),
@@ -449,7 +471,7 @@
             pltpu.VMEM((GROUPS, slots, cells, lanes), F32),
             pltpu.VMEM((GROUPS, grid, 2, orbs * per, lanes), F32),
             pltpu.VMEM((ORDER - 1, slots * cells, lanes), BF16),
-            pltpu.VMEM((GROUPS, blocks * nproj, lanes), F32),
+            pltpu.VMEM((GROUPS, slots * cells, lanes), F32),
             pltpu.VMEM((grid, tall, lanes), F32),
             pltpu.VMEM((grid, tall, lanes), F32),
             pltpu.VMEM((2 * blocks * nproj, slots * cells), BF16),
@@ -457,18 +479,22 @@
             pltpu.VMEM((slots * cells, lanes), F32),
             pltpu.VMEM((slots * cells, lanes), F32),
             pltpu.VMEM((nproj, lanes), F32),
+            pltpu.VMEM((-(-macro // 1024) * 8, LANES), F32),
             pltpu.VMEM(now.shape, F32),
+            pltpu.VMEM(old.shape, F32),
             pltpu.VMEM((STEPS, 1, LANES), F32),
             pltpu.VMEM((STEPS, layers * grid, 1, LANES), F32),
             pltpu.VMEM((2, 8, lanes), F32),
             pltpu.VMEM((3, blocks * nproj // lanes, lanes, lanes), F32),
             pltpu.VMEM((planes // blocks * (cells // lanes), lanes, lanes), F32),
-            pltpu.VMEM((ORDER, slots * cells, lanes), F32),
+            pltpu.VMEM((ORDER - 1, slots * cells, lanes), F32),
+            pltpu.VMEM((layers * grid, 1, LANES), F32),
             dma(GROUPS), dma(GROUPS),
             pltpu.SemaphoreType.DMA, pltpu.SemaphoreType.DMA,
             dma(GROUPS), dma(GROUPS),
             dma(STEPS), dma(STEPS),
-            dma(6),
+            dma(8),
+            pltpu.SemaphoreType.REGULAR,
         ],
         compiler_params=pltpu.CompilerParams(
             vmem_limit_bytes=48 * 1024 * 1024, collective_id=0, has_side_effects=True
@@ -495,15 +521,13 @@
     per = wide * mine
     kinds, nproj = strengths.shape
     macro = vector_now.shape[0]
-    padded = (macro // 1024 + 1) * 1024
-    lay = lambda vector: jnp.pad(vector, (0, padded - macro)).reshape(-1, LANES)
     held = lambda array: pltpu.with_memory_space_constraint(array, pltpu.HBM)
     field, vector = propagate(
         held(material), held(proj_kind), held(point_cell), held(strengths),
         held(rows_of(projectors).reshape(kinds, nproj * per, LANES)),
         held(rows_of(local_potential)),
         held(rows_of(orbitals).reshape(2, points, orb * per, LANES)),
-        lay(vector_now), lay(vector_old),
+        held(vector_now), held(vector_old),
         2.0 / (orb * grid * mine * cells), macro, share, grid, layers, mine, own,
     )
     field = jnp.swapaxes(field.reshape(2, points, orb, wide, mine, LANES), -3, -2).reshape(orbitals.shape)

time: 76.8 us -> 75.4 us (0.982)
  no operation moved by 1% of the time
where the time goes in v4:
time: 75.4 us; the launch traced here: 75.3 us
  Pallas kernels  72.7 us (96%)
  local copies, waits for them, and re-layouts  1.92 us (3%)
    pallas_call x1, Pallas kernels, propagate(): pl.pallas_call(functools.partial(kernel, norm, macro, share, grid, layers...  72.7 us
    unnamed x2, local copies, waits for them, and re-layouts  1.92 us

profile of v4, /device:TPU:0, one launch (start us, length us, event | category | flops | bytes accessed | tf_op | source)
XLA Modules:
  0.0 75.3 jit_solution(16981640108119137807)
XLA Ops:
  0.6 72.7 %propagate.1 = (f32[2,8,256,128]{3,2,1,0:T(8,128)S(1)}, f32[16,128]{1,0:T(8,128)S(1)}) custom-call(s32[32]{0:T(128)} %material_in.1, s32[32]{0:T(128)} %kind_in.1, s32[32]{0:T(128)} %cell_in.1, f32[2,32]{1,0:T(2,128)} %strength_in.1, f32[2,128,128]{2,1,0:T(8,128)} %bitcast.25, f32[8,4,128]{2,1,0:T(4,128)} %bitcast.26, f32[2,8,256,128]{3,2,1,0:T(8,128)} %bitcast.24, ...), custom_call_target="tpu_custom_call" | custom-call | tf_op jit(solution)/shard_map/propagate/pallas_call | solution.py:455
  73.3 1.3 %copy.17 = f32[2,8,64,2,256]{4,3,2,1,0:T(2,128)} copy(f32[2,8,64,2,256]{4,3,2,1,0:T(2,128)S(1)} %bitcast.22) | data formatting | bytes 4194304
  74.7 0.6 copy.18

commit v5 on v4

--- a/solution.py
+++ b/solution.py
@@ -354,6 +354,14 @@
         + lax.broadcasted_iota(jnp.int32, vector_ref.shape, 1)
     )
 
+    def send_back(group):
+        for other in order:
+            remote(
+                land_ref.at[group, other], field_part(out_ref, group, here),
+                out_send.at[group], out_recv.at[group], (layer, other),
+            ).start()
+        own_out(group).start()
+
     def advance(step, a):
         base = 6.0 + (SPACING * SPACING) * a * a
         level_ref[...] = diag_ref[...] + base
@@ -375,12 +383,10 @@
             @pl.when(step == STEPS - 1)
             def _():
                 finish(group)
-                for other in order:
-                    remote(
-                        land_ref.at[group, other], field_part(out_ref, group, here),
-                        out_send.at[group], out_recv.at[group], (layer, other),
-                    ).start()
-                own_out(group).start()
+
+                @pl.when(group < groups - 1)
+                def _():
+                    send_back(group)
 
             return carry
 
@@ -401,6 +407,10 @@
                         row_ref.at[step], rows_ref.at[step, layer * grid + here],
                         row_send.at[step], row_recv.at[step], (storey(distance), other),
                     ).start()
+
+        @pl.when(step == STEPS - 1)
+        def _():
+            send_back(groups - 1)
 
         @pl.when(step == 0)
         def _():

time: 75.4 us -> 74.6 us (0.989)
  Pallas kernels: 72.7 us -> 71.8 us
    pallas_call x1, Pallas kernels: 72.7 us -> 71.8 us  [propagate(): pl.pallas_call(functools.partial(kernel, norm, macro, share, grid, layers...]
where the time goes in v5:
time: 74.6 us; the launch traced here: 74.4 us
  Pallas kernels  71.8 us (96%)
  local copies, waits for them, and re-layouts  1.92 us (3%)
    pallas_call x1, Pallas kernels, propagate(): pl.pallas_call(functools.partial(kernel, norm, macro, share, grid, layers...  71.8 us
    unnamed x2, local copies, waits for them, and re-layouts  1.92 us

profile of v5, /device:TPU:0, one launch (start us, length us, event | category | flops | bytes accessed | tf_op | source)
XLA Modules:
  0.0 74.4 jit_solution(6017567246318747431)
XLA Ops:
  0.6 71.8 %propagate.1 = (f32[2,8,256,128]{3,2,1,0:T(8,128)S(1)}, f32[16,128]{1,0:T(8,128)S(1)}) custom-call(s32[32]{0:T(128)} %material_in.1, s32[32]{0:T(128)} %kind_in.1, s32[32]{0:T(128)} %cell_in.1, f32[2,32]{1,0:T(2,128)} %strength_in.1, f32[2,128,128]{2,1,0:T(8,128)} %bitcast.25, f32[8,4,128]{2,1,0:T(4,128)} %bitcast.26, f32[2,8,256,128]{3,2,1,0:T(8,128)} %bitcast.24, ...), custom_call_target="tpu_custom_call" | custom-call | tf_op jit(solution)/shard_map/propagate/pallas_call | solution.py:465
  72.4 1.3 %copy.17 = f32[2,8,64,2,256]{4,3,2,1,0:T(2,128)} copy(f32[2,8,64,2,256]{4,3,2,1,0:T(2,128)S(1)} %bitcast.22) | data formatting | bytes 4194304
  73.8 0.6 copy.18

commit v6 on v5

--- a/solution.py
+++ b/solution.py
@@ -341,11 +341,11 @@
                     else:
                         top = slot * cells + y * NZ
                         parts_ref[degree - 1, top:top + NZ, :] = jnp.concatenate(fresh, axis=0).astype(BF16)
-                last = slots * cells - cells
-                if not final and slot == slots - 2:
-                    total = jnp.dot(fore_ref[:width, :last], parts_ref[degree - 1, :last, :], preferred_element_type=F32)
-                if not final and slot == slots - 1:
-                    total = total + jnp.dot(fore_ref[:width, last:], parts_ref[degree - 1, last:, :], preferred_element_type=F32)
+                if not final and slot in (slots // 2 - 1, slots - 1):
+                    first = 0 if slot < slots // 2 else slots // 2 * cells
+                    here_cells = slice(first, (slot + 1) * cells)
+                    part = jnp.dot(fore_ref[:width, here_cells], parts_ref[degree - 1, here_cells, :], preferred_element_type=F32)
+                    total = part if first == 0 else total + part
         flow_ref[0] = flow_ref[0] + flow * jnp.where(orbital_of + group * orbs < limit, sign * (0.5 / SPACING), 0.0)
         flow_ref[1] = flow_ref[1] + density * jnp.where(orbital_of + group * orbs < limit, 1.0, 0.0)
 

time: 74.6 us -> 74.4 us (level)
  no operation moved by 1% of the time
where the time goes in v6:
time: 74.4 us; the launch traced here: 74.2 us
  Pallas kernels  71.6 us (96%)
  local copies, waits for them, and re-layouts  1.92 us (3%)
    pallas_call x1, Pallas kernels, propagate(): pl.pallas_call(functools.partial(kernel, norm, macro, share, grid, layers...  71.6 us
    unnamed x2, local copies, waits for them, and re-layouts  1.92 us

profile of v6, /device:TPU:0, one launch (start us, length us, event | category | flops | bytes accessed | tf_op | source)
XLA Modules:
  0.0 74.2 jit_solution(1982503981969262828)
XLA Ops:
  0.6 71.6 %propagate.1 = (f32[2,8,256,128]{3,2,1,0:T(8,128)S(1)}, f32[16,128]{1,0:T(8,128)S(1)}) custom-call(s32[32]{0:T(128)} %material_in.1, s32[32]{0:T(128)} %kind_in.1, s32[32]{0:T(128)} %cell_in.1, f32[2,32]{1,0:T(2,128)} %strength_in.1, f32[2,128,128]{2,1,0:T(8,128)} %bitcast.25, f32[8,4,128]{2,1,0:T(4,128)} %bitcast.26, f32[2,8,256,128]{3,2,1,0:T(8,128)} %bitcast.24, ...), custom_call_target="tpu_custom_call" | custom-call | tf_op jit(solution)/shard_map/propagate/pallas_call | solution.py:465
  72.3 1.3 %copy.17 = f32[2,8,64,2,256]{4,3,2,1,0:T(2,128)} copy(f32[2,8,64,2,256]{4,3,2,1,0:T(2,128)S(1)} %bitcast.22) | data formatting | bytes 4194304
  73.6 0.6 copy.18
